TPU v7x, 256 devices: a whole 4x4x8 slice. The times are simulated.
256 devices in a mesh: tm: 64 (over z, x, core), row: 4 (over y).
Axes of the slice: x: 4, y: 4, z: 8, core: 2. Of those that a mesh axis runs over, the one named last changes fastest.
Arguments:
- filter_map: bfloat16 [1024, 256, 256], P('tm', 'row'), may hold values from -1 to 1
- filter_cov: bfloat16 [1024, 256, 256], P('tm', 'row'), may hold values from -1 to 1
- smoother_gain: bfloat16 [1024, 256, 256], P('tm', 'row'), may hold values from -1 to 1
- transition: bfloat16 [256, 256], replicated, may hold values from -0.375 to 0.375
- site_basis: bfloat16 [2048, 256], replicated, may hold values from -0.375 to 0.375
- obs_time: int32 [32768], P('tm'), may hold values from 0 to 1023, as said below
- obs_site: int32 [32768], P('tm'), may hold values from 0 to 2047
- obs_value: float32 [32768, 128], P('tm'), may hold values from -6 to 6
- obs_weight: float32 [32768], P('tm'), may hold values from 0.5 to 8
Outputs:
- smoothed: float32 [1024, 256, 128], P('tm', 'row')
Inputs may be any that keep to these rules, and one draw needn't show every extreme that they name: `obs_time`: row r has a time step from (r // 512) * 16 to (r // 512 + 1) * 16 - 1; rows are in no order of time.
All inputs are finite; a program needn't handle non-finite values.
Results may differ from a plain program's by a relative error of at most 0.0041.
Values may be sent and summed in bfloat16 or wider, within the bound.
No kernel may reach another device: no remote copies, remote signals or barrier semaphores. Data moves between devices by JAX's collectives and lax.ppermute only.
A program may use at most 128 MiB of HBM per device.

v0:
```python
import jax
import jax.numpy as jnp
from jax import lax
from jax.experimental import pallas as pl
from jax.experimental.pallas import tpu as pltpu
from jax.sharding import Mesh, PartitionSpec as P

BF = jnp.bfloat16
F32 = jnp.float32
NZ, NX, NC, NR = 8, 4, 2, 4
NQ = 4
NT = (((1,), (1,)), ((), ()))
VM = pl.BlockSpec(memory_space=pltpu.VMEM)
HB = pl.BlockSpec(memory_space=pltpu.HBM)
SM = pl.BlockSpec(memory_space=pltpu.SMEM)
AN = pl.BlockSpec(memory_space=pl.ANY)


def split(value):
    hi = value.astype(BF)
    return hi, (value - hi.astype(F32)).astype(BF)


def mm(left, right):
    return jnp.dot(left, right, preferred_element_type=F32)


def mm3(left_hi, left_lo, right_hi, right_lo):
    return mm(left_hi, right_hi) + (mm(left_hi, right_lo) + mm(left_lo, right_hi))


def push(state, weight):
    hi, lo = split(state)
    both = lax.dot_general(
        jnp.concatenate([hi, lo], axis=0), weight, NT, preferred_element_type=F32
    )
    n = state.shape[0]
    return both[:n] + both[n:]


def push2(state, weight_hi, weight_lo):
    hi, lo = split(state)
    both = lax.dot_general(
        jnp.concatenate([hi, lo], axis=0), weight_hi, NT, preferred_element_type=F32
    )
    n = state.shape[0]
    extra = lax.dot_general(hi, weight_lo, NT, preferred_element_type=F32)
    return both[:n] + (both[n:] + extra)


def coords(idx_ref):
    me = idx_ref[0]
    row = me % NR
    tm = me // NR
    return tm // (NX * NC), (tm // NC) % NX, tm % NC, row


def call(body, outs, *args, scratch=(), far_in=(), far_out=(), any_in=()):
    many = isinstance(outs, tuple)
    count = len(outs) if many else 1
    specs = tuple(HB if i in far_out else VM for i in range(count))
    far = len(far_in) + len(far_out) + len(any_in)
    if many:
        outs = tuple(
            pltpu.HBM(o.shape, o.dtype) if i in far_out else o for i, o in enumerate(outs)
        )
    args = [args[0]] + [
        pltpu.with_memory_space_constraint(a, pltpu.HBM) if i in far_in else a
        for i, a in enumerate(args[1:])
    ]
    return pl.pallas_call(
        body,
        out_shape=outs,
        in_specs=[SM]
        + [HB if i in far_in else AN if i in any_in else VM for i in range(len(args) - 1)],
        out_specs=specs if many else specs[0],
        scratch_shapes=list(scratch) + ([pltpu.SemaphoreType.DMA((far,))] if far else []),
        compiler_params=pltpu.CompilerParams(vmem_limit_bytes=16 << 20),
    )(*args)


def shape(dims, dtype):
    return jax.ShapeDtypeStruct(dims, dtype)


def drive_body(idx, basis, value, weight, time, cov, *outs):
    row = idx[0] % NR
    steps = cov.shape[0]
    weighted = (weight[...] * jnp.transpose(value[...])).astype(BF)
    local_time = time[...] - (idx[0] // NR) * steps
    half = steps // 2
    members = weighted.shape[0] // NR
    for k in range(steps):
        masked = jnp.where(local_time == k, weighted, jnp.zeros((), BF))
        info = mm(masked, basis[...]).astype(BF)
        drive = lax.dot_general(info, cov[k], NT, preferred_element_type=F32)
        w = drive.shape[1]
        lane = (k // half) * w
        for s, out in enumerate(outs):
            part = drive[0:members]
            for r in range(1, NR):
                part = jnp.where((row + s) % NR == r, drive[r * members : (r + 1) * members], part)
            out[k % half, :, lane : lane + w] = part


def assemble(row, parts, full):
    w = parts[0].shape[1]
    for s, part in enumerate(parts):
        start = pl.multiple_of(((row - s) % NR) * w, w)
        full[:, pl.ds(start, w), :] = part[...]


def tree(items, order, quads=None):
    while len(items) > 1:
        if quads is not None and len(items) == NQ:
            n = items[0][0].shape[0]
            for q, (hi, lo) in enumerate(items):
                quads[q, 0:n] = hi
                quads[q, n:] = lo
        merged = []
        for i in range(0, len(items), 2):
            left, right = order(items[i], items[i + 1])
            if left[1] is None:
                value = mm(left[0], right[0])
            else:
                value = mm3(left[0], left[1], right[0], right[1])
            merged.append(split(value))
        items = merged
    return items[0]


def later_first(a, b):
    return b, a


def earlier_first(a, b):
    return a, b


def fwd_local_body(idx, m0, m1, m2, m3, full, quads, packed):
    _, _, _, row = coords(idx)
    assemble(row, (m0, m1, m2, m3), full)
    steps, n = full.shape[0], full.shape[1]
    hi, lo = tree([(full[k], None) for k in range(steps)], later_first, quads)
    packed[0:n] = hi
    packed[n:] = lo


def fwd_drive_body(
    idx, full, quads, d0, d1, d2, d3, far_full, far_quads, far_drives, far_sums, msg,
    drv, drives, sums, sems,
):
    _, _, _, row = coords(idx)
    save_full = pltpu.make_async_copy(full, far_full, sems.at[0])
    save_full.start()
    save_quads = pltpu.make_async_copy(quads, far_quads, sems.at[2])
    save_quads.start()
    for s, part in enumerate((d0, d1, d2, d3)):
        drv[(row - s) % NR] = part[...]
    steps, n = full.shape[0], full.shape[1]
    half, w = steps // 2, n // NR
    for k in range(steps):
        lane = (k // half) * w
        drives[k] = jnp.concatenate(
            [drv[r, k % half, :, lane : lane + w] for r in range(NR)], axis=1
        )
    save_drives = pltpu.make_async_copy(drives, far_drives, sems.at[1])
    save_drives.start()
    run = steps // NQ
    chains = [drives[q * run] for q in range(NQ)]
    for j in range(1, run):
        for q in range(NQ):
            chains[q] = push(chains[q], full[q * run + j]) + drives[q * run + j]
    for q in range(NQ):
        sums[q] = chains[q]
    save_sums = pltpu.make_async_copy(sums, far_sums, sems.at[3])
    save_sums.start()
    b = chains[0]
    for q in range(1, NQ):
        b = push2(b, quads[q, 0:n], quads[q, n:]) + chains[q]
    store_pair(msg, b)
    save_full.wait()
    save_drives.wait()
    save_quads.wait()
    save_sums.wait()


def store_pair(msg, b):
    m = b.shape[0]
    hi, lo = split(b)
    msg[0:m] = hi
    msg[m:] = lo


def load_pair(msg):
    m = msg.shape[0] // 2
    return msg[0:m].astype(F32) + msg[m:].astype(F32)


def fwd_core_body(idx, own, other, b_own, b_other, far_other, far_b, keep, msg, sems):
    save_other = pltpu.make_async_copy(other, far_other, sems.at[0])
    save_b = pltpu.make_async_copy(b_other, far_b, sems.at[1])
    save_other.start()
    save_b.start()
    _, _, c, _ = coords(idx)
    n = own.shape[1]
    m = b_own.shape[0] // 2
    first = jnp.where(c == 0, own[...], other[...])
    second = jnp.where(c == 0, other[...], own[...])
    hi, lo = split(mm3(second[0:n], second[n:], first[0:n], first[n:]))
    b_mine, b_theirs = load_pair(b_own), load_pair(b_other)
    b_first = jnp.where(c == 0, b_mine, b_theirs)
    b_second = jnp.where(c == 0, b_theirs, b_mine)
    b = push2(b_first, second[0:n], second[n:]) + b_second
    w = n // NC
    keep[0:n] = hi
    keep[n : 2 * n] = lo
    b_hi, b_lo = split(b)
    keep[2 * n : 2 * n + m] = b_hi
    keep[2 * n + m :] = b_lo
    msg[0:n] = half_of(c, hi, w)
    msg[n : 2 * n] = half_of(c, lo, w)
    msg[2 * n :] = pack_vector(c, b)
    save_other.wait()
    save_b.wait()


def half_of(c, value, w):
    return jnp.where(c == 0, value[:, :w], value[:, w:])


def pack_vector(c, b):
    m, n = b.shape
    w, q = n // NC, m // NC
    hi, lo = split(jnp.where(c == 0, b[:q], b[q:]))
    return jnp.concatenate([hi[:, :w], hi[:, w:], lo[:, :w], lo[:, w:]], axis=0)


def unpack_part(msg, at, q):
    p = [msg[at + j * q : at + (j + 1) * q].astype(F32) for j in range(4)]
    return jnp.concatenate([p[0] + p[2], p[1] + p[3]], axis=1)


def unpack_vector(c, mine, other, at, m):
    q = m // NC
    a, b = unpack_part(mine, at, q), unpack_part(other, at, q)
    return jnp.concatenate([jnp.where(c == 0, a, b), jnp.where(c == 0, b, a)], axis=0)


def join(c, mine, other, rows):
    a, b = mine[0:rows], other[0:rows]
    return jnp.concatenate([jnp.where(c == 0, a, b), jnp.where(c == 0, b, a)], axis=1)


def fwd_x_body(idx, own, r1, r2, r3, s1, s2, s3, far_ax, far_bx, msg, ax, bx, sems):
    _, x, c, _ = coords(idx)
    rows, n = ax.shape[1:]
    m = bx.shape[1]
    for s, (mine, other) in enumerate(((own, None), (r1, s1), (r2, s2), (r3, s3))):
        at = (x - s) % NX
        if other is None:
            ax[at] = mine[0:rows]
            bx[at] = mine[rows : rows + m].astype(F32) + mine[rows + m :].astype(F32)
        else:
            ax[at] = join(c, mine, other, rows)
            bx[at] = unpack_vector(c, mine, other, rows, m)
    save_ax = pltpu.make_async_copy(ax, far_ax, sems.at[0])
    save_bx = pltpu.make_async_copy(bx, far_bx, sems.at[1])
    save_ax.start()
    save_bx.start()
    hi, _ = tree([(ax[i, 0:n], ax[i, n:]) for i in range(NX)], later_first)
    b = bx[0]
    for i in range(1, NX):
        b = push2(b, ax[i, 0:n], ax[i, n:]) + bx[i]
    hi = half_of(c, hi, n // NC)
    packed = pack_vector(c, b)
    for i in range(NZ):
        msg[i, 0:n] = hi
        msg[i, n:] = packed
    save_ax.wait()
    save_bx.wait()


def bwd_local_body(idx, g0, g1, g2, g3, full, quads, packed, sems):
    _, _, _, row = coords(idx)
    steps, n = full.shape[0], full.shape[1]
    w = n // NR
    copies = []
    for s, part in enumerate((g0, g1, g2, g3)):
        start = pl.multiple_of(((row - s) % NR) * w, w)
        copies.append(
            pltpu.make_async_copy(part, full.at[:, pl.ds(start, w), :], sems.at[s])
        )
        copies[-1].start()
    for copy in copies:
        copy.wait()

    @pl.when(idx[0] // NR == NZ * NX * NC - 1)
    def _():
        full[steps - 1] = jnp.zeros((n, n), BF)

    hi, lo = tree([(full[k], None) for k in range(steps)], earlier_first, quads)
    packed[0:n] = hi
    packed[n:] = lo


def bwd_core_body(idx, own, other, out, msg):
    _, _, c, _ = coords(idx)
    n = own.shape[1]
    first = jnp.where(c == 0, own[...], other[...])
    second = jnp.where(c == 0, other[...], own[...])
    hi, lo = split(mm3(first[0:n], first[n:], second[0:n], second[n:]))
    out[0:n] = hi
    out[n:] = lo
    msg[0:n] = half_of(c, hi, n // NC)
    msg[n:] = half_of(c, lo, n // NC)


def bwd_x_body(idx, own, r1, r2, r3, s1, s2, s3, far_cx, msg, cx, sems):
    _, x, c, _ = coords(idx)
    rows, n = own.shape
    cx[x] = own[...]
    for s, mine, other in ((1, r1, s1), (2, r2, s2), (3, r3, s3)):
        cx[(x - s) % NX] = join(c, mine, other, rows)
    save_cx = pltpu.make_async_copy(cx, far_cx, sems.at[0])
    save_cx.start()
    hi, _ = tree([(cx[i, 0:n], cx[i, n:]) for i in range(NX)], earlier_first)
    hi = half_of(c, hi, n // NC)
    for i in range(NZ):
        msg[i] = hi
    save_cx.wait()


def load(sems, at, *pairs):
    copies = []
    for i, (far, close) in enumerate(pairs):
        copy = pltpu.make_async_copy(far, close, sems.at[at + i])
        copy.start()
        copies.append(copy)
    return copies


def fetch_body(idx, gains, quads, far, far_gains, far_quads, out, sems):
    save_quads = pltpu.make_async_copy(quads, far_quads, sems.at[2])
    save_quads.start()
    copy = pltpu.make_async_copy(far, out, sems.at[0])
    save = pltpu.make_async_copy(gains, far_gains, sems.at[1])
    save.start()
    copy.start()
    copy.wait()
    save.wait()
    save_quads.wait()


def filter_body(
    idx, mine, swapped, b_other, far_other, far_transition, far_ax, far_bx, far_quads, far_sums,
    far_full, far_drives, far_gains, far_cquads, far_off, far_fsums, msg,
    other, transition, ax, bx, quads, sums, full, drives, gains, cquads, off, fsums, sems,
):
    z, x, c, _ = coords(idx)
    steps, n = full.shape[0], full.shape[1]
    m = drives.shape[1]
    run = steps // NQ
    (
        get_ax, get_bx, get_other, get_quads, get_sums, get_drives, get_full, get_transition,
        get_gains, get_cquads,
    ) = load(
        sems, 0, (far_ax.at[pl.ds(0, NX - 1)], ax), (far_bx, bx), (far_other, other),
        (far_quads.at[pl.ds(0, NQ - 1)], quads),
        (far_sums, sums), (far_drives, drives), (far_full, full), (far_transition, transition),
        (far_gains, gains), (far_cquads.at[pl.ds(0, NQ - 1)], cquads),
    )
    state = jnp.zeros((m, n), F32)
    for i in range(NZ - 1):
        b = unpack_vector(c, mine.at[i], swapped.at[i], n, m)
        moved = push(state, join(c, mine.at[i], swapped.at[i], n)) + b
        state = jnp.where(i < z, moved, state)
    get_ax.wait()
    get_bx.wait()
    for i in range(NX - 1):
        moved = push2(state, ax[i, 0:n], ax[i, n:]) + bx[i]
        state = jnp.where(i < x, moved, state)
    get_other.wait()
    moved = push2(state, other[0:n], other[n:]) + load_pair(b_other)
    state = jnp.where(c == 1, moved, state)
    get_quads.wait()
    get_sums.wait()
    chains = [state]
    for q in range(NQ - 1):
        chains.append(push2(chains[q], quads[q, 0:n], quads[q, n:]) + sums[q])
    get_drives.wait()
    get_full.wait()
    for j in range(run):
        for q in range(NQ):
            k = q * run + j
            chains[q] = push(chains[q], full[k]) + drives[k]
            off[k] = chains[q]
    get_transition.wait()
    weight = transition[...]
    get_gains.wait()
    moved = push(off[...].reshape(steps * m, n), weight)
    for k in range(steps):
        off[k] = off[k] - push(moved[k * m : (k + 1) * m], gains[k])
    save_off = pltpu.make_async_copy(off, far_off, sems.at[10])
    save_off.start()
    chains = [off[q * run + run - 1] for q in range(NQ)]
    for j in range(run - 2, -1, -1):
        for q in range(NQ):
            k = q * run + j
            chains[q] = push(chains[q], gains[k]) + off[k]
    for q in range(NQ):
        fsums[q] = chains[q]
    save_fsums = pltpu.make_async_copy(fsums, far_fsums, sems.at[11])
    save_fsums.start()
    get_cquads.wait()
    f = chains[NQ - 1]
    for q in range(NQ - 2, -1, -1):
        f = push2(f, cquads[q, 0:n], cquads[q, n:]) + chains[q]
    store_pair(msg, f)
    save_off.wait()
    save_fsums.wait()


def back_core_body(idx, own, other, cown, cother, out):
    _, _, c, _ = coords(idx)
    n = own.shape[1]
    f_own, f_other = load_pair(own), load_pair(other)
    f0 = jnp.where(c == 0, f_own, f_other)
    f1 = jnp.where(c == 0, f_other, f_own)
    hi = jnp.where(c == 0, cown[0:n], cother[0:n])
    lo = jnp.where(c == 0, cown[n:], cother[n:])
    out[...] = push2(f1, hi, lo) + f0


def back_x_body(idx, f0, f1, f2, f3, far_cx, fx, out, cx, sems):
    (get_cx,) = load(sems, 0, (far_cx, cx))
    _, x, _, _ = coords(idx)
    n = fx.shape[2]
    for s, part in enumerate((f0, f1, f2, f3)):
        fx[(x - s) % NX] = part[...]
    get_cx.wait()
    f = fx[NX - 1]
    for i in range(NX - 2, -1, -1):
        f = push2(f, cx[i, 0:n], cx[i, n:]) + fx[i]
    for i in range(NZ):
        out[i] = f


def smooth_body(
    idx, mine, swapped, fz, fx, fother, cother, far_cx, far_quads, far_sums, far_gains, far_off,
    o0, o1, o2, o3, cx, quads, sums, gains, off, sems,
):
    get_cx, get_quads, get_sums, get_gains, get_off = load(
        sems, 0, (far_cx, cx), (far_quads, quads), (far_sums, sums), (far_gains, gains),
        (far_off, off),
    )
    z, x, c, row = coords(idx)
    steps, n = gains.shape[0], gains.shape[1]
    m = off.shape[1]
    half, w = steps // 2, n // NR
    state = jnp.zeros((m, n), F32)
    for i in range(NZ - 1, 0, -1):
        moved = push(state, join(c, mine.at[i], swapped.at[i], n)) + fz[i].astype(F32)
        state = jnp.where(i > z, moved, state)
    get_cx.wait()
    for i in range(NX - 1, 0, -1):
        moved = push2(state, cx[i, 0:n], cx[i, n:]) + fx[i]
        state = jnp.where(i > x, moved, state)
    moved = push2(state, cother[0:n], cother[n:]) + load_pair(fother)
    state = jnp.where(c == 0, moved, state)
    get_quads.wait()
    get_sums.wait()
    chains = [state] * NQ
    for q in range(NQ - 1, 0, -1):
        chains[q - 1] = push2(chains[q], quads[q, 0:n], quads[q, n:]) + sums[q]
    get_gains.wait()
    get_off.wait()
    run = steps // NQ
    for j in range(run - 1, -1, -1):
        for q in range(NQ):
            k = q * run + j
            chains[q] = push(chains[q], gains[k]) + off[k]
            lane = (k // half) * w
            parts = [chains[q][:, r * w : (r + 1) * w].astype(BF) for r in range(NR)]
            for s, out in enumerate((o0, o1, o2, o3)):
                part = parts[0]
                for r in range(1, NR):
                    part = jnp.where((row + s) % NR == r, parts[r], part)
                out[k % half, :, lane : lane + w] = part


def place_body(idx, p0, p1, p2, p3, out, got):
    _, _, _, row = coords(idx)
    half = out.shape[0] // 2
    w = out.shape[1]
    for s, part in enumerate((p0, p1, p2, p3)):
        got[(row - s) % NR] = part[...]
    for k in range(half):
        block = jnp.concatenate([got[r, k] for r in range(NR)], axis=0).astype(F32)
        turned = jnp.transpose(block)
        out[k] = turned[:w]
        out[k + half] = turned[w:]


def shift(value, axis, step, size):
    return lax.ppermute(value, axis, [(i, (i + step) % size) for i in range(size)])


def spread(value, axis):
    return lax.all_to_all(value, axis, 0, 0, tiled=True)


def swap(value):
    return lax.ppermute(value, "c", [(0, 1), (1, 0)])


def gather_rows(value):
    return [value] + [shift(value, "row", s, NR) for s in range(1, NR)]


def local(
    filter_map,
    filter_cov,
    smoother_gain,
    transition,
    site_basis,
    obs_time,
    obs_site,
    obs_value,
    obs_weight,
):
    steps, w, n = filter_map.shape
    obs, members = obs_value.shape
    m = members // NR
    half = steps // 2
    tm = (lax.axis_index("z") * NX + lax.axis_index("x")) * NC + lax.axis_index("c")
    idx = (tm * NR + lax.axis_index("row")).astype(jnp.int32).reshape(1)

    maps = gather_rows(filter_map)
    basis_rows = site_basis.at[obs_site].get(mode="promise_in_bounds")
    drive = call(
        drive_body,
        (shape((half, m, 2 * w), F32),) * NR,
        idx,
        basis_rows,
        obs_value,
        obs_weight.reshape(1, obs),
        obs_time.reshape(1, obs),
        filter_cov,
    )
    gain_in, _ = lax.optimization_barrier((smoother_gain, drive))
    drive = drive[:1] + tuple(shift(drive[s], "row", s, NR) for s in range(1, NR))
    gains = gather_rows(gain_in)
    full, quads, packed = call(
        fwd_local_body,
        (shape((steps, n, n), BF), shape((NQ, 2 * n, n), BF), shape((2 * n, n), BF)),
        idx,
        *maps,
    )
    packed_other = swap(packed)
    full, quads, drives, sums, bmsg = call(
        fwd_drive_body,
        (
            shape((steps, n, n), BF),
            shape((NQ, 2 * n, n), BF),
            shape((steps, m, n), F32),
            shape((NQ, m, n), F32),
            shape((2 * m, n), BF),
        ),
        idx,
        full,
        quads,
        *drive,
        scratch=[
            pltpu.VMEM((NR, half, m, 2 * w), F32),
            pltpu.VMEM((steps, m, n), F32),
            pltpu.VMEM((NQ, m, n), F32),
        ],
        far_out=(0, 1, 2, 3),
    )
    bmsg_other = swap(bmsg)
    far_other, far_b, keep, msg = call(
        fwd_core_body,
        (
            shape((2 * n, n), BF),
            shape((2 * m, n), BF),
            shape((2 * n + 2 * m, n), BF),
            shape((2 * n + 2 * m, n // NC), BF),
        ),
        idx,
        packed,
        packed_other,
        bmsg,
        bmsg_other,
        far_out=(0, 1),
    )
    got = [shift(msg, "x", s, NX) for s in range(1, NX)]
    ax, bx, msg = call(
        fwd_x_body,
        (
            shape((NX, 2 * n, n), BF),
            shape((NX, m, n), F32),
            shape((NZ, n + 2 * m, n // NC), BF),
        ),
        idx,
        keep,
        *got,
        *[swap(g) for g in got],
        scratch=[pltpu.VMEM((NX, 2 * n, n), BF), pltpu.VMEM((NX, m, n), F32)],
        far_out=(0, 1),
    )
    up = spread(msg, "z")

    gains, _ = lax.optimization_barrier((gains, msg))
    gfull, cquads, cpacked = call(
        bwd_local_body,
        (shape((steps, n, n), BF), shape((NQ, 2 * n, n), BF), shape((2 * n, n), BF)),
        idx,
        *gains,
        any_in=(0, 1, 2, 3),
    )
    cother = swap(cpacked)
    c32, cmsg = call(
        bwd_core_body,
        (shape((2 * n, n), BF), shape((2 * n, n // NC), BF)),
        idx,
        cpacked,
        cother,
    )
    got = [shift(cmsg, "x", s, NX) for s in range(1, NX)]
    cx, cmsg = call(
        bwd_x_body,
        (shape((NX, 2 * n, n), BF), shape((NZ, n, n // NC), BF)),
        idx,
        c32,
        *got,
        *[swap(g) for g in got],
        scratch=[pltpu.VMEM((NX, 2 * n, n), BF)],
        far_out=(0,),
    )
    down = spread(cmsg, "z")
    gfull, cquads, b_other = call(
        fetch_body,
        (shape((steps, n, n), BF), shape((NQ, 2 * n, n), BF), shape((2 * m, n), BF)),
        idx,
        gfull,
        cquads,
        far_b,
        far_in=(2,),
        far_out=(0, 1),
    )
    up_other = swap(up)
    off, fsums, fmsg = call(
        filter_body,
        (shape((steps, m, n), F32), shape((NQ, m, n), F32), shape((2 * m, n), BF)),
        idx,
        up,
        up_other,
        b_other,
        far_other,
        transition,
        ax,
        bx,
        quads,
        sums,
        full,
        drives,
        gfull,
        cquads,
        scratch=[
            pltpu.VMEM((2 * n, n), BF),
            pltpu.VMEM((n, n), BF),
            pltpu.VMEM((NX - 1, 2 * n, n), BF),
            pltpu.VMEM((NX, m, n), F32),
            pltpu.VMEM((NQ - 1, 2 * n, n), BF),
            pltpu.VMEM((NQ, m, n), F32),
            pltpu.VMEM((steps, n, n), BF),
            pltpu.VMEM((steps, m, n), F32),
            pltpu.VMEM((steps, n, n), BF),
            pltpu.VMEM((NQ - 1, 2 * n, n), BF),
            pltpu.VMEM((steps, m, n), F32),
            pltpu.VMEM((NQ, m, n), F32),
        ],
        far_in=(3, 4, 5, 6, 7, 8, 9, 10, 11, 12),
        far_out=(0, 1),
    )
    fother = swap(fmsg)
    f = call(back_core_body, shape((m, n), F32), idx, fmsg, fother, cpacked, cother)
    fx, f = call(
        back_x_body,
        (shape((NX, m, n), F32), shape((NZ, m, n), F32)),
        idx,
        f,
        *[shift(f, "x", s, NX) for s in range(1, NX)],
        cx,
        scratch=[pltpu.VMEM((NX, 2 * n, n), BF)],
        far_in=(4,),
    )
    fz = spread(f, "z")
    out = call(
        smooth_body,
        (shape((half, m, 2 * w), BF),) * NR,
        idx,
        down,
        swap(down),
        fz,
        fx,
        fother,
        cother,
        cx,
        cquads,
        fsums,
        gfull,
        off,
        scratch=[
            pltpu.VMEM((NX, 2 * n, n), BF),
            pltpu.VMEM((NQ, 2 * n, n), BF),
            pltpu.VMEM((NQ, m, n), F32),
            pltpu.VMEM((steps, n, n), BF),
            pltpu.VMEM((steps, m, n), F32),
        ],
        far_in=(6, 7, 8, 9, 10),
    )
    out = out[:1] + tuple(shift(out[s], "row", s, NR) for s in range(1, NR))
    return call(
        place_body,
        shape((steps, w, members), F32),
        idx,
        *out,
        scratch=[pltpu.VMEM((NR, half, m, 2 * w), BF)],
    )


def solution(mesh):
    fine = Mesh(mesh.devices.reshape(NZ, NX, NC, NR), ("z", "x", "c", "row"))
    t = ("z", "x", "c")
    placed = (
        P(t, "row", None),
        P(t, "row", None),
        P(t, "row", None),
        P(),
        P(),
        P(t),
        P(t),
        P(t, None),
        P(t),
    )

    return jax.shard_map(
        local, mesh=fine, in_specs=placed, out_specs=P(t, "row", None), check_vma=False
    )
```

profile of v0, /device:TPU:1, one launch (start us, length us, event | category | flops | bytes accessed | tf_op | source)
XLA Modules:
  0.0 192.5 jit_solution(670092787742135884)
XLA Ops:
  0.0 2.1 %collective-permute-start.3 = (bf16[16,64,256]{2,1,0:T(8,128)(2,1)}, bf16[16,64,256]{2,1,0:T(8,128)(2,1)S(1)}, u32[]{:S(2)}, u32[]{:S(2)}) collective-permute-start(bf16[16,64,256]{2,1,0:T(8,128)(2,1)} %m0.1), channel_id=1, source_target_pairs={{0,1},{1,2},{2,3},{3,0},{4,5},{5,6},{6,7},{7,4},{8,9},{9,10},{10,1... | collective-permute-start | bytes 1572872 | tf_op jit(solution)/shard_map/ppermute | solution.py:506
  2.1 2.6 %collective-permute-start.4 = (bf16[16,64,256]{2,1,0:T(8,128)(2,1)}, bf16[16,64,256]{2,1,0:T(8,128)(2,1)S(1)}, u32[]{:S(2)}, u32[]{:S(2)}) collective-permute-start(bf16[16,64,256]{2,1,0:T(8,128)(2,1)} %m0.1), channel_id=1, source_target_pairs={{0,2},{1,3},{2,0},{3,1},{4,6},{5,7},{6,4},{7,5},{8,10},{9,11},{10,... | collective-permute-start | bytes 1572872 | tf_op jit(solution)/shard_map/ppermute | solution.py:506
  6.5 7.0 %collective-permute-done.3.m1 = bf16[16,64,256]{2,1,0:T(8,128)(2,1)S(1)} collective-permute-done((bf16[16,64,256]{2,1,0:T(8,128)(2,1)}, bf16[16,64,256]{2,1,0:T(8,128)(2,1)S(1)}, u32[]{:S(2)}, u32[]{:S(2)}) %collective-permute-start.3) | collective-permute-done | bytes 524320 | tf_op jit(solution)/shard_map/ppermute | solution.py:506
  14.3 13.3 %collective-permute-done.4.m2 = bf16[16,64,256]{2,1,0:T(8,128)(2,1)S(1)} collective-permute-done((bf16[16,64,256]{2,1,0:T(8,128)(2,1)}, bf16[16,64,256]{2,1,0:T(8,128)(2,1)S(1)}, u32[]{:S(2)}, u32[]{:S(2)}) %collective-permute-start.4) | collective-permute-done | bytes 524320 | tf_op jit(solution)/shard_map/ppermute | solution.py:506
  33.3 2.3 %shard_map.92 = (bf16[16,256,256]{2,1,0:T(8,128)(2,1)S(1)}, bf16[4,512,256]{2,1,0:T(8,128)(2,1)S(1)}, bf16[512,256]{1,0:T(8,128)(2,1)}) custom-call(s32[1]{0:T(128)} %bitcast.idx, bf16[16,64,256]{2,1,0:T(8,128)(2,1)S(1)} %copy-done.7, bf16[16,64,256]{2,1,0:T(8,128)(2,1)S(1)} %copy-done.10, bf16[16,64,256]{2,1,0:T(8,128)(2,1)S(1)} %copy-done.12, ...), custom_call_target="tpu_custom_call" | custom-call | tf_op jit(solution)/shard_map/pallas_call | solution.py:71
  38.2 2.0 %gather_fusion = bf16[512,256]{1,0:T(8,128)(2,1)S(1)} fusion(bf16[2048,256]{1,0:T(8,128)(2,1)S(1)} %copy-done, s32[1024]{0:T(1024)S(1)} %pad_clamp_fusion), kind=kCustom, calls=%fused_computation | custom fusion | bytes 526336 | tf_op jit(solution)/shard_map/gather | solution.py:540
  42.2 3.1 %shard_map.91 = (f32[8,32,128]{2,1,0:T(8,128)S(1)}, f32[8,32,128]{2,1,0:T(8,128)S(1)}, f32[8,32,128]{2,1,0:T(8,128)S(1)}, f32[8,32,128]{2,1,0:T(8,128)S(1)}) custom-call(s32[1]{0:T(128)} %bitcast.idx, bf16[512,256]{1,0:T(8,128)(2,1)S(1)} %gather_fusion, f32[512,128]{1,0:T(8,128)S(1)} %copy-done.16, f32[1,512]{1,0:T(1,128)S(1)} %bitcast.3, ...), custom_call_target="tpu_custom_call" | custom-call | tf_op jit(solution)/shard_map/pallas_call | solution.py:71
  45.6 2.1 %collective-permute-start.8 = (f32[8,32,128]{2,1,0:T(8,128)S(1)}, f32[8,32,128]{2,1,0:T(8,128)S(1)}, u32[]{:S(2)}, u32[]{:S(2)}) collective-permute-start(f32[8,32,128]{2,1,0:T(8,128)S(1)} %get-tuple-element.50), channel_id=1, source_target_pairs={{0,2},{1,3},{2,0},{3,1},{4,6},{5,7},{6,4},{7,5},{8,10},{9,11},{10,... | collective-permute-start | bytes 393224 | tf_op jit(solution)/shard_map/ppermute | solution.py:506
  49.0 3.1 %collective-permute-done.7.d1 = f32[8,32,128]{2,1,0:T(8,128)S(1)} collective-permute-done((f32[8,32,128]{2,1,0:T(8,128)S(1)}, f32[8,32,128]{2,1,0:T(8,128)S(1)}, u32[]{:S(2)}, u32[]{:S(2)}) %collective-permute-start.7) | collective-permute-done | bytes 131104 | tf_op jit(solution)/shard_map/ppermute | solution.py:506
  52.1 2.0 %collective-permute-done.8.d2 = f32[8,32,128]{2,1,0:T(8,128)S(1)} collective-permute-done((f32[8,32,128]{2,1,0:T(8,128)S(1)}, f32[8,32,128]{2,1,0:T(8,128)S(1)}, u32[]{:S(2)}, u32[]{:S(2)}) %collective-permute-start.8) | collective-permute-done | bytes 131104 | tf_op jit(solution)/shard_map/ppermute | solution.py:506
  56.0 2.0 %shard_map.93 = (bf16[16,256,256]{2,1,0:T(8,128)(2,1)}, bf16[4,512,256]{2,1,0:T(8,128)(2,1)}, f32[16,32,256]{2,1,0:T(8,128)}, f32[4,32,256]{2,1,0:T(8,128)}, bf16[64,256]{1,0:T(8,128)(2,1)S(1)}) custom-call(s32[1]{0:T(128)} %bitcast.idx, bf16[16,256,256]{2,1,0:T(8,128)(2,1)S(1)} %get-tuple-element.54.full, bf16[4,512,256]{2,1,0:T(8,128)(2,1)S(1)} %copy-done.6, ...), custom_call_target="tpu_custom_call" | custom-call | tf_op jit(solution)/shard_map/pallas_call | solution.py:71
  63.1 2.5 %collective-permute-start.12 = (bf16[576,128]{1,0:T(8,128)(2,1)S(1)}, bf16[576,128]{1,0:T(8,128)(2,1)S(1)}, u32[]{:S(2)}, u32[]{:S(2)}) collective-permute-start(bf16[576,128]{1,0:T(8,128)(2,1)S(1)} %get-tuple-element.58), channel_id=1, source_target_pairs={{0,16},{8,24},{16,0},{24,8},{1,17},{9,25},{17,1},{25,9},{2,18},{10... | collective-permute-start | bytes 442376 | tf_op jit(solution)/shard_map/ppermute | solution.py:506
  69.4 2.9 %collective-permute-done.12.r2 = bf16[576,128]{1,0:T(8,128)(2,1)S(1)} collective-permute-done((bf16[576,128]{1,0:T(8,128)(2,1)S(1)}, bf16[576,128]{1,0:T(8,128)(2,1)S(1)}, u32[]{:S(2)}, u32[]{:S(2)}) %collective-permute-start.12) | collective-permute-done | bytes 147488 | tf_op jit(solution)/shard_map/ppermute | solution.py:506
  74.9 2.3 %shard_map.95 = (bf16[4,512,256]{2,1,0:T(8,128)(2,1)}, f32[4,32,256]{2,1,0:T(8,128)}, bf16[8,320,128]{2,1,0:T(8,128)(2,1)}) custom-call(s32[1]{0:T(128)} %bitcast.idx, bf16[576,256]{1,0:T(8,128)(2,1)S(1)} %get-tuple-element.57.own, bf16[576,128]{1,0:T(8,128)(2,1)S(1)} %collective-permute-done.11.r1, bf16[576,128]{1,0:T(8,128)(2,1)S(1)} %collective-permute-done.12.r2, ...), custom_call_target="tpu_custom_call" | custom-call | tf_op jit(solution)/shard_map/pallas_call | solution.py:71
  77.3 8.2 %all-to-all-start.1 = ((bf16[8,320,128]{2,1,0:T(8,128)(2,1)}), bf16[8,320,128]{2,1,0:T(8,128)(2,1)S(1)}, u32[]{:S(2)}, u32[]{:S(2)}) async-start(bf16[8,320,128]{2,1,0:T(8,128)(2,1)} %get-tuple-element.59), calls=%async_computation.1 | async-start | bytes 1310720 | tf_op jit(solution)/shard_map/all_to_all | solution.py:510
  86.5 2.7 %collective-permute-start.1 = (bf16[16,64,256]{2,1,0:T(8,128)(2,1)S(1)}, bf16[16,64,256]{2,1,0:T(8,128)(2,1)S(1)}, u32[]{:S(2)}, u32[]{:S(2)}) collective-permute-start(bf16[16,64,256]{2,1,0:T(8,128)(2,1)S(1)} %copy-done.8), channel_id=1, source_target_pairs={{0,2},{1,3},{2,0},{3,1},{4,6},{5,7},{6,4},{7,5},{8,10},{9,11},{10,... | collective-permute-start | bytes 1572872 | tf_op jit(solution)/shard_map/ppermute | solution.py:506
  89.1 10.6 %collective-permute-done.g1 = bf16[16,64,256]{2,1,0:T(8,128)(2,1)S(1)} collective-permute-done((bf16[16,64,256]{2,1,0:T(8,128)(2,1)S(1)}, bf16[16,64,256]{2,1,0:T(8,128)(2,1)S(1)}, u32[]{:S(2)}, u32[]{:S(2)}) %collective-permute-start) | collective-permute-done | bytes 524320 | tf_op jit(solution)/shard_map/ppermute | solution.py:506
  99.8 12.1 %collective-permute-done.1.g2 = bf16[16,64,256]{2,1,0:T(8,128)(2,1)S(1)} collective-permute-done((bf16[16,64,256]{2,1,0:T(8,128)(2,1)S(1)}, bf16[16,64,256]{2,1,0:T(8,128)(2,1)S(1)}, u32[]{:S(2)}, u32[]{:S(2)}) %collective-permute-start.1) | collective-permute-done | bytes 524320 | tf_op jit(solution)/shard_map/ppermute | solution.py:506
  111.9 1.8 shard_map.96
  119.7 2.1 %collective-permute-start.19 = (bf16[512,128]{1,0:T(8,128)(2,1)S(1)}, bf16[512,128]{1,0:T(8,128)(2,1)S(1)}, u32[]{:S(2)}, u32[]{:S(2)}) collective-permute-start(bf16[512,128]{1,0:T(8,128)(2,1)S(1)} %get-tuple-element.66), channel_id=1, source_target_pairs={{0,16},{8,24},{16,0},{24,8},{1,17},{9,25},{17,1},{25,9},{2,18},{10... | collective-permute-start | bytes 393224 | tf_op jit(solution)/shard_map/ppermute | solution.py:506
  123.1 1.8 collective-permute-done.18.r1
  124.9 1.9 %collective-permute-start.21 = (bf16[512,128]{1,0:T(8,128)(2,1)S(1)}, bf16[512,128]{1,0:T(8,128)(2,1)S(1)}, u32[]{:S(2)}, u32[]{:S(2)}) collective-permute-start(bf16[512,128]{1,0:T(8,128)(2,1)S(1)} %collective-permute-done.18.r1), channel_id=1, source_target_pairs={{0,4},{4,0},{1,5},{5,1},{2,6},{6,2},{3,7},{7,3},{8,12},{12,8},{9,1... | collective-permute-start | bytes 393224 | tf_op jit(solution)/shard_map/ppermute | solution.py:514
  130.5 2.0 %shard_map.98 = (bf16[4,512,256]{2,1,0:T(8,128)(2,1)}, bf16[8,256,128]{2,1,0:T(8,128)(2,1)}) custom-call(s32[1]{0:T(128)} %bitcast.idx, bf16[512,256]{1,0:T(8,128)(2,1)S(1)} %get-tuple-element.65.own, bf16[512,128]{1,0:T(8,128)(2,1)S(1)} %collective-permute-done.18.r1, bf16[512,128]{1,0:T(8,128)(2,1)S(1)} %collective-permute-done.19.r2, ...), custom_call_target="tpu_custom_call" | custom-call | tf_op jit(solution)/shard_map/pallas_call | solution.py:71
  132.5 6.6 %all-to-all-start = ((bf16[8,256,128]{2,1,0:T(8,128)(2,1)}), bf16[8,256,128]{2,1,0:T(8,128)(2,1)S(1)}, u32[]{:S(2)}, u32[]{:S(2)}) async-start(bf16[8,256,128]{2,1,0:T(8,128)(2,1)} %get-tuple-element.67), calls=%async_computation | async-start | bytes 1048576 | tf_op jit(solution)/shard_map/all_to_all | solution.py:510
  144.4 6.4 %shard_map.100 = (f32[16,32,256]{2,1,0:T(8,128)}, f32[4,32,256]{2,1,0:T(8,128)}, bf16[64,256]{1,0:T(8,128)(2,1)S(1)}) custom-call(s32[1]{0:T(128)} %bitcast.idx, bf16[8,320,128]{2,1,0:T(8,128)(2,1)S(1)} %all-to-all-done.1.mine, bf16[8,320,128]{2,1,0:T(8,128)(2,1)S(1)} %collective-permute-done.25.swapped, bf16[64,256]{1,0:T(8,128)(2,1)S(1)} %get-tuple-element.71.b_other, ...), custom_call_target="tpu_custom_call" | custom-call | tf_op jit(solution)/shard_map/pallas_call | solution.py:71
  150.9 6.1 %all-to-all-done.mine = bf16[8,256,128]{2,1,0:T(8,128)(2,1)S(1)} async-done(((bf16[8,256,128]{2,1,0:T(8,128)(2,1)}), bf16[8,256,128]{2,1,0:T(8,128)(2,1)S(1)}, u32[]{:S(2)}, u32[]{:S(2)}) %all-to-all-start) | async-done | bytes 524320 | tf_op jit(solution)/shard_map/all_to_all | solution.py:510
  159.3 2.2 %collective-permute-start.28 = (f32[32,256]{1,0:T(8,128)S(1)}, f32[32,256]{1,0:T(8,128)S(1)}, u32[]{:S(2)}, u32[]{:S(2)}) collective-permute-start(f32[32,256]{1,0:T(8,128)S(1)} %shard_map.101.f0), channel_id=1, source_target_pairs={{0,16},{8,24},{16,0},{24,8},{1,17},{9,25},{17,1},{25,9},{2,18},{10... | collective-permute-start | bytes 98312 | tf_op jit(solution)/shard_map/ppermute | solution.py:506
  164.5 2.5 %shard_map.102 = (f32[4,32,256]{2,1,0:T(8,128)S(1)}, f32[8,32,256]{2,1,0:T(8,128)}) custom-call(s32[1]{0:T(128)} %bitcast.idx, f32[32,256]{1,0:T(8,128)S(1)} %shard_map.101.f0, f32[32,256]{1,0:T(8,128)S(1)} %collective-permute-done.27.f1, f32[32,256]{1,0:T(8,128)S(1)} %collective-permute-done.28.f2, f32[32,256]{1,0:T(8,128)S(1)} %collective-permute-done.29.f3, ...), custom_call_target="tpu_custom_call" | custom-call | tf_op jit(solution)/shard_map/pallas_call | solution.py:71
  167.0 3.4 %all-to-all-start.2 = ((f32[8,32,256]{2,1,0:T(8,128)}), f32[8,32,256]{2,1,0:T(8,128)S(1)}, u32[]{:S(2)}, u32[]{:S(2)}) async-start(f32[8,32,256]{2,1,0:T(8,128)} %get-tuple-element.83), calls=%async_computation.2 | async-start | bytes 524288 | tf_op jit(solution)/shard_map/all_to_all | solution.py:510
  170.5 10.1 %all-to-all-done.2.fz = f32[8,32,256]{2,1,0:T(8,128)S(1)} async-done(((f32[8,32,256]{2,1,0:T(8,128)}), f32[8,32,256]{2,1,0:T(8,128)S(1)}, u32[]{:S(2)}, u32[]{:S(2)}) %all-to-all-start.2) | async-done | bytes 262176 | tf_op jit(solution)/shard_map/all_to_all | solution.py:510
  180.6 4.5 %shard_map.103 = (bf16[8,32,128]{2,1,0:T(8,128)(2,1)S(1)}, bf16[8,32,128]{2,1,0:T(8,128)(2,1)S(1)}, bf16[8,32,128]{2,1,0:T(8,128)(2,1)S(1)}, bf16[8,32,128]{2,1,0:T(8,128)(2,1)S(1)}) custom-call(s32[1]{0:T(128)} %bitcast.idx, bf16[8,256,128]{2,1,0:T(8,128)(2,1)S(1)} %all-to-all-done.mine, bf16[8,256,128]{2,1,0:T(8,128)(2,1)S(1)} %collective-permute-done.24.swapped, ...), custom_call_target="tpu_custom_call" | custom-call | tf_op jit(solution)/shard_map/pallas_call | solution.py:71
  185.8 2.7 %collective-permute-start.31 = (bf16[8,32,128]{2,1,0:T(8,128)(2,1)S(1)}, bf16[8,32,128]{2,1,0:T(8,128)(2,1)S(1)}, u32[]{:S(2)}, u32[]{:S(2)}) collective-permute-start(bf16[8,32,128]{2,1,0:T(8,128)(2,1)S(1)} %get-tuple-element.89), channel_id=1, source_target_pairs={{0,2},{1,3},{2,0},{3,1},{4,6},{5,7},{6,4},{7,5},{8,10},{9,11},{10,... | collective-permute-start | bytes 196616 | tf_op jit(solution)/shard_map/ppermute | solution.py:506
  (95 shorter events, 55.0 us)
Async XLA Ops:
  0.0 13.5 %collective-permute-start.3 = (bf16[16,64,256]{2,1,0:T(8,128)(2,1)}, bf16[16,64,256]{2,1,0:T(8,128)(2,1)S(1)}, u32[]{:S(2)}, u32[]{:S(2)}) collective-permute-start(bf16[16,64,256]{2,1,0:T(8,128)(2,1)} %m0.1), channel_id=1, source_target_pairs={{0,1},{1,2},{2,3},{3,0},{4,5},{5,6},{6,7},{7,4},{8,9},{9,10},{10,1... | collective-permute-start | bytes 1572872 | tf_op jit(solution)/shard_map/ppermute | solution.py:506
  2.1 25.4 %collective-permute-start.4 = (bf16[16,64,256]{2,1,0:T(8,128)(2,1)}, bf16[16,64,256]{2,1,0:T(8,128)(2,1)S(1)}, u32[]{:S(2)}, u32[]{:S(2)}) collective-permute-start(bf16[16,64,256]{2,1,0:T(8,128)(2,1)} %m0.1), channel_id=1, source_target_pairs={{0,2},{1,3},{2,0},{3,1},{4,6},{5,7},{6,4},{7,5},{8,10},{9,11},{10,... | collective-permute-start | bytes 1572872 | tf_op jit(solution)/shard_map/ppermute | solution.py:506
  4.7 23.6 %collective-permute-start.5 = (bf16[16,64,256]{2,1,0:T(8,128)(2,1)}, bf16[16,64,256]{2,1,0:T(8,128)(2,1)S(1)}, u32[]{:S(2)}, u32[]{:S(2)}) collective-permute-start(bf16[16,64,256]{2,1,0:T(8,128)(2,1)} %m0.1), channel_id=1, source_target_pairs={{0,3},{1,0},{2,1},{3,2},{4,7},{5,4},{6,5},{7,6},{8,11},{9,8},{10,9... | collective-permute-start | bytes 1572872 | tf_op jit(solution)/shard_map/ppermute | solution.py:506
  36.7 23.4 %collective-permute-start.6 = (bf16[512,256]{1,0:T(8,128)(2,1)}, bf16[512,256]{1,0:T(8,128)(2,1)}, u32[]{:S(2)}, u32[]{:S(2)}) collective-permute-start(bf16[512,256]{1,0:T(8,128)(2,1)} %get-tuple-element.53.own), channel_id=1, source_target_pairs={{0,4},{4,0},{1,5},{5,1},{2,6},{6,2},{3,7},{7,3},{8,12},{12,8},{9,1... | collective-permute-start | bytes 786440 | tf_op jit(solution)/shard_map/ppermute | solution.py:514
  45.3 6.8 %collective-permute-start.7 = (f32[8,32,128]{2,1,0:T(8,128)S(1)}, f32[8,32,128]{2,1,0:T(8,128)S(1)}, u32[]{:S(2)}, u32[]{:S(2)}) collective-permute-start(f32[8,32,128]{2,1,0:T(8,128)S(1)} %get-tuple-element.49), channel_id=1, source_target_pairs={{0,1},{1,2},{2,3},{3,0},{4,5},{5,6},{6,7},{7,4},{8,9},{9,10},{10,1... | collective-permute-start | bytes 393224 | tf_op jit(solution)/shard_map/ppermute | solution.py:506
  45.6 8.5 %collective-permute-start.8 = (f32[8,32,128]{2,1,0:T(8,128)S(1)}, f32[8,32,128]{2,1,0:T(8,128)S(1)}, u32[]{:S(2)}, u32[]{:S(2)}) collective-permute-start(f32[8,32,128]{2,1,0:T(8,128)S(1)} %get-tuple-element.50), channel_id=1, source_target_pairs={{0,2},{1,3},{2,0},{3,1},{4,6},{5,7},{6,4},{7,5},{8,10},{9,11},{10,... | collective-permute-start | bytes 393224 | tf_op jit(solution)/shard_map/ppermute | solution.py:506
  47.7 7.1 %collective-permute-start.9 = (f32[8,32,128]{2,1,0:T(8,128)S(1)}, f32[8,32,128]{2,1,0:T(8,128)S(1)}, u32[]{:S(2)}, u32[]{:S(2)}) collective-permute-start(f32[8,32,128]{2,1,0:T(8,128)S(1)} %get-tuple-element.51), channel_id=1, source_target_pairs={{0,3},{1,0},{2,1},{3,2},{4,7},{5,4},{6,5},{7,6},{8,11},{9,8},{10,9... | collective-permute-start | bytes 393224 | tf_op jit(solution)/shard_map/ppermute | solution.py:506
  61.9 6.3 %collective-permute-start.11 = (bf16[576,128]{1,0:T(8,128)(2,1)S(1)}, bf16[576,128]{1,0:T(8,128)(2,1)S(1)}, u32[]{:S(2)}, u32[]{:S(2)}) collective-permute-start(bf16[576,128]{1,0:T(8,128)(2,1)S(1)} %get-tuple-element.58), channel_id=1, source_target_pairs={{0,8},{8,16},{16,24},{24,0},{1,9},{9,17},{17,25},{25,1},{2,10},{10... | collective-permute-start | bytes 442376 | tf_op jit(solution)/shard_map/ppermute | solution.py:506
  63.1 9.2 %collective-permute-start.12 = (bf16[576,128]{1,0:T(8,128)(2,1)S(1)}, bf16[576,128]{1,0:T(8,128)(2,1)S(1)}, u32[]{:S(2)}, u32[]{:S(2)}) collective-permute-start(bf16[576,128]{1,0:T(8,128)(2,1)S(1)} %get-tuple-element.58), channel_id=1, source_target_pairs={{0,16},{8,24},{16,0},{24,8},{1,17},{9,25},{17,1},{25,9},{2,18},{10... | collective-permute-start | bytes 442376 | tf_op jit(solution)/shard_map/ppermute | solution.py:506
  65.6 8.0 %collective-permute-start.13 = (bf16[576,128]{1,0:T(8,128)(2,1)S(1)}, bf16[576,128]{1,0:T(8,128)(2,1)S(1)}, u32[]{:S(2)}, u32[]{:S(2)}) collective-permute-start(bf16[576,128]{1,0:T(8,128)(2,1)S(1)} %get-tuple-element.58), channel_id=1, source_target_pairs={{0,24},{8,0},{16,8},{24,16},{1,25},{9,1},{17,9},{25,17},{2,26},{10... | collective-permute-start | bytes 442376 | tf_op jit(solution)/shard_map/ppermute | solution.py:506
  68.2 5.4 %collective-permute-start.14 = (bf16[576,128]{1,0:T(8,128)(2,1)S(1)}, bf16[576,128]{1,0:T(8,128)(2,1)S(1)}, u32[]{:S(2)}, u32[]{:S(2)}) collective-permute-start(bf16[576,128]{1,0:T(8,128)(2,1)S(1)} %collective-permute-done.11.r1), channel_id=1, source_target_pairs={{0,4},{4,0},{1,5},{5,1},{2,6},{6,2},{3,7},{7,3},{8,12},{12,8},{9,1... | collective-permute-start | bytes 442376 | tf_op jit(solution)/shard_map/ppermute | solution.py:514
  77.3 55.3 %all-to-all-start.1 = ((bf16[8,320,128]{2,1,0:T(8,128)(2,1)}), bf16[8,320,128]{2,1,0:T(8,128)(2,1)S(1)}, u32[]{:S(2)}, u32[]{:S(2)}) async-start(bf16[8,320,128]{2,1,0:T(8,128)(2,1)} %get-tuple-element.59), calls=%async_computation.1 | async-start | bytes 1310720 | tf_op jit(solution)/shard_map/all_to_all | solution.py:510
  85.5 14.3 %collective-permute-start = (bf16[16,64,256]{2,1,0:T(8,128)(2,1)S(1)}, bf16[16,64,256]{2,1,0:T(8,128)(2,1)S(1)}, u32[]{:S(2)}, u32[]{:S(2)}) collective-permute-start(bf16[16,64,256]{2,1,0:T(8,128)(2,1)S(1)} %copy-done.8), channel_id=1, source_target_pairs={{0,1},{1,2},{2,3},{3,0},{4,5},{5,6},{6,7},{7,4},{8,9},{9,10},{10,1... | collective-permute-start | bytes 1572872 | tf_op jit(solution)/shard_map/ppermute | solution.py:506
  86.5 25.5 %collective-permute-start.1 = (bf16[16,64,256]{2,1,0:T(8,128)(2,1)S(1)}, bf16[16,64,256]{2,1,0:T(8,128)(2,1)S(1)}, u32[]{:S(2)}, u32[]{:S(2)}) collective-permute-start(bf16[16,64,256]{2,1,0:T(8,128)(2,1)S(1)} %copy-done.8), channel_id=1, source_target_pairs={{0,2},{1,3},{2,0},{3,1},{4,6},{5,7},{6,4},{7,5},{8,10},{9,11},{10,... | collective-permute-start | bytes 1572872 | tf_op jit(solution)/shard_map/ppermute | solution.py:506
  89.1 22.8 %collective-permute-start.2 = (bf16[16,64,256]{2,1,0:T(8,128)(2,1)S(1)}, bf16[16,64,256]{2,1,0:T(8,128)(2,1)S(1)}, u32[]{:S(2)}, u32[]{:S(2)}) collective-permute-start(bf16[16,64,256]{2,1,0:T(8,128)(2,1)S(1)} %copy-done.8), channel_id=1, source_target_pairs={{0,3},{1,0},{2,1},{3,2},{4,7},{5,4},{6,5},{7,6},{8,11},{9,8},{10,9... | collective-permute-start | bytes 1572872 | tf_op jit(solution)/shard_map/ppermute | solution.py:506
  116.1 2.5 %collective-permute-start.17 = (bf16[512,256]{1,0:T(8,128)(2,1)S(1)}, bf16[512,256]{1,0:T(8,128)(2,1)S(1)}, u32[]{:S(2)}, u32[]{:S(2)}) collective-permute-start(bf16[512,256]{1,0:T(8,128)(2,1)S(1)} %get-tuple-element.64.own.cown), channel_id=1, source_target_pairs={{0,4},{4,0},{1,5},{5,1},{2,6},{6,2},{3,7},{7,3},{8,12},{12,8},{9,1... | collective-permute-start | bytes 786440 | tf_op jit(solution)/shard_map/ppermute | solution.py:514
  118.9 6.0 %collective-permute-start.18 = (bf16[512,128]{1,0:T(8,128)(2,1)S(1)}, bf16[512,128]{1,0:T(8,128)(2,1)S(1)}, u32[]{:S(2)}, u32[]{:S(2)}) collective-permute-start(bf16[512,128]{1,0:T(8,128)(2,1)S(1)} %get-tuple-element.66), channel_id=1, source_target_pairs={{0,8},{8,16},{16,24},{24,0},{1,9},{9,17},{17,25},{25,1},{2,10},{10... | collective-permute-start | bytes 393224 | tf_op jit(solution)/shard_map/ppermute | solution.py:506
  119.7 8.1 %collective-permute-start.19 = (bf16[512,128]{1,0:T(8,128)(2,1)S(1)}, bf16[512,128]{1,0:T(8,128)(2,1)S(1)}, u32[]{:S(2)}, u32[]{:S(2)}) collective-permute-start(bf16[512,128]{1,0:T(8,128)(2,1)S(1)} %get-tuple-element.66), channel_id=1, source_target_pairs={{0,16},{8,24},{16,0},{24,8},{1,17},{9,25},{17,1},{25,9},{2,18},{10... | collective-permute-start | bytes 393224 | tf_op jit(solution)/shard_map/ppermute | solution.py:506
  121.8 7.3 %collective-permute-start.20 = (bf16[512,128]{1,0:T(8,128)(2,1)S(1)}, bf16[512,128]{1,0:T(8,128)(2,1)S(1)}, u32[]{:S(2)}, u32[]{:S(2)}) collective-permute-start(bf16[512,128]{1,0:T(8,128)(2,1)S(1)} %get-tuple-element.66), channel_id=1, source_target_pairs={{0,24},{8,0},{16,8},{24,16},{1,25},{9,1},{17,9},{25,17},{2,26},{10... | collective-permute-start | bytes 393224 | tf_op jit(solution)/shard_map/ppermute | solution.py:506
  124.9 4.6 %collective-permute-start.21 = (bf16[512,128]{1,0:T(8,128)(2,1)S(1)}, bf16[512,128]{1,0:T(8,128)(2,1)S(1)}, u32[]{:S(2)}, u32[]{:S(2)}) collective-permute-start(bf16[512,128]{1,0:T(8,128)(2,1)S(1)} %collective-permute-done.18.r1), channel_id=1, source_target_pairs={{0,4},{4,0},{1,5},{5,1},{2,6},{6,2},{3,7},{7,3},{8,12},{12,8},{9,1... | collective-permute-start | bytes 393224 | tf_op jit(solution)/shard_map/ppermute | solution.py:514
  127.8 2.2 %collective-permute-start.22 = (bf16[512,128]{1,0:T(8,128)(2,1)S(1)}, bf16[512,128]{1,0:T(8,128)(2,1)S(1)}, u32[]{:S(2)}, u32[]{:S(2)}) collective-permute-start(bf16[512,128]{1,0:T(8,128)(2,1)S(1)} %collective-permute-done.19.r2), channel_id=1, source_target_pairs={{0,4},{4,0},{1,5},{5,1},{2,6},{6,2},{3,7},{7,3},{8,12},{12,8},{9,1... | collective-permute-start | bytes 393224 | tf_op jit(solution)/shard_map/ppermute | solution.py:514
  132.5 24.5 %all-to-all-start = ((bf16[8,256,128]{2,1,0:T(8,128)(2,1)}), bf16[8,256,128]{2,1,0:T(8,128)(2,1)S(1)}, u32[]{:S(2)}, u32[]{:S(2)}) async-start(bf16[8,256,128]{2,1,0:T(8,128)(2,1)} %get-tuple-element.67), calls=%async_computation | async-start | bytes 1048576 | tf_op jit(solution)/shard_map/all_to_all | solution.py:510
  139.1 5.3 %collective-permute-start.25 = (bf16[8,320,128]{2,1,0:T(8,128)(2,1)S(1)}, bf16[8,320,128]{2,1,0:T(8,128)(2,1)S(1)}, u32[]{:S(2)}, u32[]{:S(2)}) collective-permute-start(bf16[8,320,128]{2,1,0:T(8,128)(2,1)S(1)} %all-to-all-done.1.mine), channel_id=1, source_target_pairs={{0,4},{4,0},{1,5},{5,1},{2,6},{6,2},{3,7},{7,3},{8,12},{12,8},{9,1... | collective-permute-start | bytes 1966088 | tf_op jit(solution)/shard_map/ppermute | solution.py:514
  150.8 6.7 %collective-permute-start.26 = (bf16[64,256]{1,0:T(8,128)(2,1)S(1)}, bf16[64,256]{1,0:T(8,128)(2,1)S(1)}, u32[]{:S(2)}, u32[]{:S(2)}) collective-permute-start(bf16[64,256]{1,0:T(8,128)(2,1)S(1)} %get-tuple-element.81.own), channel_id=1, source_target_pairs={{0,4},{4,0},{1,5},{5,1},{2,6},{6,2},{3,7},{7,3},{8,12},{12,8},{9,1... | collective-permute-start | bytes 98312 | tf_op jit(solution)/shard_map/ppermute | solution.py:514
  157.1 13.4 %collective-permute-start.24 = (bf16[8,256,128]{2,1,0:T(8,128)(2,1)S(1)}, bf16[8,256,128]{2,1,0:T(8,128)(2,1)S(1)}, u32[]{:S(2)}, u32[]{:S(2)}) collective-permute-start(bf16[8,256,128]{2,1,0:T(8,128)(2,1)S(1)} %all-to-all-done.mine), channel_id=1, source_target_pairs={{0,4},{4,0},{1,5},{5,1},{2,6},{6,2},{3,7},{7,3},{8,12},{12,8},{9,1... | collective-permute-start | bytes 1572872 | tf_op jit(solution)/shard_map/ppermute | solution.py:514
  157.8 4.2 %collective-permute-start.27 = (f32[32,256]{1,0:T(8,128)S(1)}, f32[32,256]{1,0:T(8,128)S(1)}, u32[]{:S(2)}, u32[]{:S(2)}) collective-permute-start(f32[32,256]{1,0:T(8,128)S(1)} %shard_map.101.f0), channel_id=1, source_target_pairs={{0,8},{8,16},{16,24},{24,0},{1,9},{9,17},{17,25},{25,1},{2,10},{10... | collective-permute-start | bytes 98312 | tf_op jit(solution)/shard_map/ppermute | solution.py:506
  159.3 4.3 %collective-permute-start.28 = (f32[32,256]{1,0:T(8,128)S(1)}, f32[32,256]{1,0:T(8,128)S(1)}, u32[]{:S(2)}, u32[]{:S(2)}) collective-permute-start(f32[32,256]{1,0:T(8,128)S(1)} %shard_map.101.f0), channel_id=1, source_target_pairs={{0,16},{8,24},{16,0},{24,8},{1,17},{9,25},{17,1},{25,9},{2,18},{10... | collective-permute-start | bytes 98312 | tf_op jit(solution)/shard_map/ppermute | solution.py:506
  161.4 3.1 %collective-permute-start.29 = (f32[32,256]{1,0:T(8,128)S(1)}, f32[32,256]{1,0:T(8,128)S(1)}, u32[]{:S(2)}, u32[]{:S(2)}) collective-permute-start(f32[32,256]{1,0:T(8,128)S(1)} %shard_map.101.f0), channel_id=1, source_target_pairs={{0,24},{8,0},{16,8},{24,16},{1,25},{9,1},{17,9},{25,17},{2,26},{10... | collective-permute-start | bytes 98312 | tf_op jit(solution)/shard_map/ppermute | solution.py:506
  167.0 13.6 %all-to-all-start.2 = ((f32[8,32,256]{2,1,0:T(8,128)}), f32[8,32,256]{2,1,0:T(8,128)S(1)}, u32[]{:S(2)}, u32[]{:S(2)}) async-start(f32[8,32,256]{2,1,0:T(8,128)} %get-tuple-element.83), calls=%async_computation.2 | async-start | bytes 524288 | tf_op jit(solution)/shard_map/all_to_all | solution.py:510
  185.1 4.4 %collective-permute-start.30 = (bf16[8,32,128]{2,1,0:T(8,128)(2,1)S(1)}, bf16[8,32,128]{2,1,0:T(8,128)(2,1)S(1)}, u32[]{:S(2)}, u32[]{:S(2)}) collective-permute-start(bf16[8,32,128]{2,1,0:T(8,128)(2,1)S(1)} %get-tuple-element.88), channel_id=1, source_target_pairs={{0,1},{1,2},{2,3},{3,0},{4,5},{5,6},{6,7},{7,4},{8,9},{9,10},{10,1... | collective-permute-start | bytes 196616 | tf_op jit(solution)/shard_map/ppermute | solution.py:506
  185.8 5.0 %collective-permute-start.31 = (bf16[8,32,128]{2,1,0:T(8,128)(2,1)S(1)}, bf16[8,32,128]{2,1,0:T(8,128)(2,1)S(1)}, u32[]{:S(2)}, u32[]{:S(2)}) collective-permute-start(bf16[8,32,128]{2,1,0:T(8,128)(2,1)S(1)} %get-tuple-element.89), channel_id=1, source_target_pairs={{0,2},{1,3},{2,0},{3,1},{4,6},{5,7},{6,4},{7,5},{8,10},{9,11},{10,... | collective-permute-start | bytes 196616 | tf_op jit(solution)/shard_map/ppermute | solution.py:506
  188.4 3.1 %collective-permute-start.32 = (bf16[8,32,128]{2,1,0:T(8,128)(2,1)S(1)}, bf16[8,32,128]{2,1,0:T(8,128)(2,1)S(1)}, u32[]{:S(2)}, u32[]{:S(2)}) collective-permute-start(bf16[8,32,128]{2,1,0:T(8,128)(2,1)S(1)} %get-tuple-element.90), channel_id=1, source_target_pairs={{0,3},{1,0},{2,1},{3,2},{4,7},{5,4},{6,5},{7,6},{8,11},{9,8},{10,9... | collective-permute-start | bytes 196616 | tf_op jit(solution)/shard_map/ppermute | solution.py:506
  (23 other events, 102.6 us)
where the time goes:
time: 195 us; the launch traced here: 193 us
  waiting for transfers between devices  82.3 us (42%)
  starting transfers between devices  59.3 us (30%)
  Pallas kernels  32.1 us (16%)
  local copies, waits for them, and re-layouts  17.9 us (9%)
    ppermute x21, waiting for transfers between devices, shift(): lax.ppermute(value, axis, [(i, (i + step) % size) for i in range(size)])  61.6 us
    pallas_call x14, Pallas kernels, call(): pl.pallas_call(body, out_shape=outs, in_specs=[SM] + [HB if i in far_in e...  32.1 us
    ppermute x21, starting transfers between devices, shift(): lax.ppermute(value, axis, [(i, (i + step) % size) for i in range(size)])  29.7 us
    all_to_all x3, starting transfers between devices, spread(): return lax.all_to_all(value, axis, 0, 0, tiled=True)  18.2 us
    all_to_all x3, waiting for transfers between devices, spread(): return lax.all_to_all(value, axis, 0, 0, tiled=True)  16.3 us
    unnamed x38, local copies, waits for them, and re-layouts  16 us
    ppermute x12, starting transfers between devices, swap(): return lax.ppermute(value, 'c', [(0, 1), (1, 0)])  11.4 us
    ppermute x12, waiting for transfers between devices, swap(): return lax.ppermute(value, 'c', [(0, 1), (1, 0)])  4.38 us
  transfers between devices with their start and end apart: 36, of which 24 were waited for; matrix products, arithmetic and copies ran while one was open for 1% of the time, Pallas kernels for 10%

commit v1 on v0

--- a/solution.py
+++ b/solution.py
@@ -481,7 +481,7 @@
             k = q * run + j
             chains[q] = push(chains[q], gains[k]) + off[k]
             lane = (k // half) * w
-            parts = [chains[q][:, r * w : (r + 1) * w].astype(BF) for r in range(NR)]
+            parts = [chains[q][:, r * w : (r + 1) * w] for r in range(NR)]
             for s, out in enumerate((o0, o1, o2, o3)):
                 part = parts[0]
                 for r in range(1, NR):
@@ -496,7 +496,7 @@
     for s, part in enumerate((p0, p1, p2, p3)):
         got[(row - s) % NR] = part[...]
     for k in range(half):
-        block = jnp.concatenate([got[r, k] for r in range(NR)], axis=0).astype(F32)
+        block = jnp.concatenate([got[r, k] for r in range(NR)], axis=0)
         turned = jnp.transpose(block)
         out[k] = turned[:w]
         out[k + half] = turned[w:]
@@ -699,7 +699,7 @@
     fz = spread(f, "z")
     out = call(
         smooth_body,
-        (shape((half, m, 2 * w), BF),) * NR,
+        (shape((half, m, 2 * w), F32),) * NR,
         idx,
         down,
         swap(down),
@@ -727,7 +727,7 @@
         shape((steps, w, members), F32),
         idx,
         *out,
-        scratch=[pltpu.VMEM((NR, half, m, 2 * w), BF)],
+        scratch=[pltpu.VMEM((NR, half, m, 2 * w), F32)],
     )
 
 

time: 195 us -> 196 us (level)
  no operation moved by 1% of the time
where the time goes in v1:
time: 196 us; the launch traced here: 194 us
  waiting for transfers between devices  83.2 us (42%)
  starting transfers between devices  59.3 us (30%)
  Pallas kernels  32.3 us (16%)
  local copies, waits for them, and re-layouts  17.9 us (9%)
    ppermute x21, waiting for transfers between devices, shift(): lax.ppermute(value, axis, [(i, (i + step) % size) for i in range(size)])  62.6 us
    pallas_call x14, Pallas kernels, call(): pl.pallas_call(body, out_shape=outs, in_specs=[SM] + [HB if i in far_in e...  32.3 us
    ppermute x21, starting transfers between devices, shift(): lax.ppermute(value, axis, [(i, (i + step) % size) for i in range(size)])  29.7 us
    all_to_all x3, starting transfers between devices, spread(): return lax.all_to_all(value, axis, 0, 0, tiled=True)  18.2 us
    all_to_all x3, waiting for transfers between devices, spread(): return lax.all_to_all(value, axis, 0, 0, tiled=True)  16.3 us
    unnamed x38, local copies, waits for them, and re-layouts  16 us
    ppermute x12, starting transfers between devices, swap(): return lax.ppermute(value, 'c', [(0, 1), (1, 0)])  11.4 us
    ppermute x12, waiting for transfers between devices, swap(): return lax.ppermute(value, 'c', [(0, 1), (1, 0)])  4.38 us
  transfers between devices with their start and end apart: 36, of which 24 were waited for; matrix products, arithmetic and copies ran while one was open for 1% of the time, Pallas kernels for 10%

profile of v1, /device:TPU:1, one launch (start us, length us, event | category | flops | bytes accessed | tf_op | source)
XLA Modules:
  0.0 193.7 jit_solution(15508307677218011081)
XLA Ops:
  0.0 2.1 %collective-permute-start.3 = (bf16[16,64,256]{2,1,0:T(8,128)(2,1)}, bf16[16,64,256]{2,1,0:T(8,128)(2,1)S(1)}, u32[]{:S(2)}, u32[]{:S(2)}) collective-permute-start(bf16[16,64,256]{2,1,0:T(8,128)(2,1)} %m0.1), channel_id=1, source_target_pairs={{0,1},{1,2},{2,3},{3,0},{4,5},{5,6},{6,7},{7,4},{8,9},{9,10},{10,1... | collective-permute-start | bytes 1572872 | tf_op jit(solution)/shard_map/ppermute | solution.py:506
  2.1 2.6 %collective-permute-start.4 = (bf16[16,64,256]{2,1,0:T(8,128)(2,1)}, bf16[16,64,256]{2,1,0:T(8,128)(2,1)S(1)}, u32[]{:S(2)}, u32[]{:S(2)}) collective-permute-start(bf16[16,64,256]{2,1,0:T(8,128)(2,1)} %m0.1), channel_id=1, source_target_pairs={{0,2},{1,3},{2,0},{3,1},{4,6},{5,7},{6,4},{7,5},{8,10},{9,11},{10,... | collective-permute-start | bytes 1572872 | tf_op jit(solution)/shard_map/ppermute | solution.py:506
  6.5 7.0 %collective-permute-done.3.m1 = bf16[16,64,256]{2,1,0:T(8,128)(2,1)S(1)} collective-permute-done((bf16[16,64,256]{2,1,0:T(8,128)(2,1)}, bf16[16,64,256]{2,1,0:T(8,128)(2,1)S(1)}, u32[]{:S(2)}, u32[]{:S(2)}) %collective-permute-start.3) | collective-permute-done | bytes 524320 | tf_op jit(solution)/shard_map/ppermute | solution.py:506
  14.3 13.3 %collective-permute-done.4.m2 = bf16[16,64,256]{2,1,0:T(8,128)(2,1)S(1)} collective-permute-done((bf16[16,64,256]{2,1,0:T(8,128)(2,1)}, bf16[16,64,256]{2,1,0:T(8,128)(2,1)S(1)}, u32[]{:S(2)}, u32[]{:S(2)}) %collective-permute-start.4) | collective-permute-done | bytes 524320 | tf_op jit(solution)/shard_map/ppermute | solution.py:506
  33.3 2.3 %shard_map.92 = (bf16[16,256,256]{2,1,0:T(8,128)(2,1)S(1)}, bf16[4,512,256]{2,1,0:T(8,128)(2,1)S(1)}, bf16[512,256]{1,0:T(8,128)(2,1)}) custom-call(s32[1]{0:T(128)} %bitcast.idx, bf16[16,64,256]{2,1,0:T(8,128)(2,1)S(1)} %copy-done.7, bf16[16,64,256]{2,1,0:T(8,128)(2,1)S(1)} %copy-done.10, bf16[16,64,256]{2,1,0:T(8,128)(2,1)S(1)} %copy-done.12, ...), custom_call_target="tpu_custom_call" | custom-call | tf_op jit(solution)/shard_map/pallas_call | solution.py:71
  38.2 2.0 %gather_fusion = bf16[512,256]{1,0:T(8,128)(2,1)S(1)} fusion(bf16[2048,256]{1,0:T(8,128)(2,1)S(1)} %copy-done, s32[1024]{0:T(1024)S(1)} %pad_clamp_fusion), kind=kCustom, calls=%fused_computation | custom fusion | bytes 526336 | tf_op jit(solution)/shard_map/gather | solution.py:540
  42.2 3.1 %shard_map.91 = (f32[8,32,128]{2,1,0:T(8,128)S(1)}, f32[8,32,128]{2,1,0:T(8,128)S(1)}, f32[8,32,128]{2,1,0:T(8,128)S(1)}, f32[8,32,128]{2,1,0:T(8,128)S(1)}) custom-call(s32[1]{0:T(128)} %bitcast.idx, bf16[512,256]{1,0:T(8,128)(2,1)S(1)} %gather_fusion, f32[512,128]{1,0:T(8,128)S(1)} %copy-done.16, f32[1,512]{1,0:T(1,128)S(1)} %bitcast.3, ...), custom_call_target="tpu_custom_call" | custom-call | tf_op jit(solution)/shard_map/pallas_call | solution.py:71
  45.6 2.1 %collective-permute-start.8 = (f32[8,32,128]{2,1,0:T(8,128)S(1)}, f32[8,32,128]{2,1,0:T(8,128)S(1)}, u32[]{:S(2)}, u32[]{:S(2)}) collective-permute-start(f32[8,32,128]{2,1,0:T(8,128)S(1)} %get-tuple-element.50), channel_id=1, source_target_pairs={{0,2},{1,3},{2,0},{3,1},{4,6},{5,7},{6,4},{7,5},{8,10},{9,11},{10,... | collective-permute-start | bytes 393224 | tf_op jit(solution)/shard_map/ppermute | solution.py:506
  49.0 3.1 %collective-permute-done.7.d1 = f32[8,32,128]{2,1,0:T(8,128)S(1)} collective-permute-done((f32[8,32,128]{2,1,0:T(8,128)S(1)}, f32[8,32,128]{2,1,0:T(8,128)S(1)}, u32[]{:S(2)}, u32[]{:S(2)}) %collective-permute-start.7) | collective-permute-done | bytes 131104 | tf_op jit(solution)/shard_map/ppermute | solution.py:506
  52.1 2.0 %collective-permute-done.8.d2 = f32[8,32,128]{2,1,0:T(8,128)S(1)} collective-permute-done((f32[8,32,128]{2,1,0:T(8,128)S(1)}, f32[8,32,128]{2,1,0:T(8,128)S(1)}, u32[]{:S(2)}, u32[]{:S(2)}) %collective-permute-start.8) | collective-permute-done | bytes 131104 | tf_op jit(solution)/shard_map/ppermute | solution.py:506
  56.0 2.0 %shard_map.93 = (bf16[16,256,256]{2,1,0:T(8,128)(2,1)}, bf16[4,512,256]{2,1,0:T(8,128)(2,1)}, f32[16,32,256]{2,1,0:T(8,128)}, f32[4,32,256]{2,1,0:T(8,128)}, bf16[64,256]{1,0:T(8,128)(2,1)S(1)}) custom-call(s32[1]{0:T(128)} %bitcast.idx, bf16[16,256,256]{2,1,0:T(8,128)(2,1)S(1)} %get-tuple-element.54.full, bf16[4,512,256]{2,1,0:T(8,128)(2,1)S(1)} %copy-done.6, ...), custom_call_target="tpu_custom_call" | custom-call | tf_op jit(solution)/shard_map/pallas_call | solution.py:71
  63.1 2.5 %collective-permute-start.12 = (bf16[576,128]{1,0:T(8,128)(2,1)S(1)}, bf16[576,128]{1,0:T(8,128)(2,1)S(1)}, u32[]{:S(2)}, u32[]{:S(2)}) collective-permute-start(bf16[576,128]{1,0:T(8,128)(2,1)S(1)} %get-tuple-element.58), channel_id=1, source_target_pairs={{0,16},{8,24},{16,0},{24,8},{1,17},{9,25},{17,1},{25,9},{2,18},{10... | collective-permute-start | bytes 442376 | tf_op jit(solution)/shard_map/ppermute | solution.py:506
  69.4 2.9 %collective-permute-done.12.r2 = bf16[576,128]{1,0:T(8,128)(2,1)S(1)} collective-permute-done((bf16[576,128]{1,0:T(8,128)(2,1)S(1)}, bf16[576,128]{1,0:T(8,128)(2,1)S(1)}, u32[]{:S(2)}, u32[]{:S(2)}) %collective-permute-start.12) | collective-permute-done | bytes 147488 | tf_op jit(solution)/shard_map/ppermute | solution.py:506
  74.9 2.3 %shard_map.95 = (bf16[4,512,256]{2,1,0:T(8,128)(2,1)}, f32[4,32,256]{2,1,0:T(8,128)}, bf16[8,320,128]{2,1,0:T(8,128)(2,1)}) custom-call(s32[1]{0:T(128)} %bitcast.idx, bf16[576,256]{1,0:T(8,128)(2,1)S(1)} %get-tuple-element.57.own, bf16[576,128]{1,0:T(8,128)(2,1)S(1)} %collective-permute-done.11.r1, bf16[576,128]{1,0:T(8,128)(2,1)S(1)} %collective-permute-done.12.r2, ...), custom_call_target="tpu_custom_call" | custom-call | tf_op jit(solution)/shard_map/pallas_call | solution.py:71
  77.3 8.2 %all-to-all-start.1 = ((bf16[8,320,128]{2,1,0:T(8,128)(2,1)}), bf16[8,320,128]{2,1,0:T(8,128)(2,1)S(1)}, u32[]{:S(2)}, u32[]{:S(2)}) async-start(bf16[8,320,128]{2,1,0:T(8,128)(2,1)} %get-tuple-element.59), calls=%async_computation.1 | async-start | bytes 1310720 | tf_op jit(solution)/shard_map/all_to_all | solution.py:510
  86.5 2.7 %collective-permute-start.1 = (bf16[16,64,256]{2,1,0:T(8,128)(2,1)S(1)}, bf16[16,64,256]{2,1,0:T(8,128)(2,1)S(1)}, u32[]{:S(2)}, u32[]{:S(2)}) collective-permute-start(bf16[16,64,256]{2,1,0:T(8,128)(2,1)S(1)} %copy-done.8), channel_id=1, source_target_pairs={{0,2},{1,3},{2,0},{3,1},{4,6},{5,7},{6,4},{7,5},{8,10},{9,11},{10,... | collective-permute-start | bytes 1572872 | tf_op jit(solution)/shard_map/ppermute | solution.py:506
  89.1 10.6 %collective-permute-done.g1 = bf16[16,64,256]{2,1,0:T(8,128)(2,1)S(1)} collective-permute-done((bf16[16,64,256]{2,1,0:T(8,128)(2,1)S(1)}, bf16[16,64,256]{2,1,0:T(8,128)(2,1)S(1)}, u32[]{:S(2)}, u32[]{:S(2)}) %collective-permute-start) | collective-permute-done | bytes 524320 | tf_op jit(solution)/shard_map/ppermute | solution.py:506
  99.8 12.1 %collective-permute-done.1.g2 = bf16[16,64,256]{2,1,0:T(8,128)(2,1)S(1)} collective-permute-done((bf16[16,64,256]{2,1,0:T(8,128)(2,1)S(1)}, bf16[16,64,256]{2,1,0:T(8,128)(2,1)S(1)}, u32[]{:S(2)}, u32[]{:S(2)}) %collective-permute-start.1) | collective-permute-done | bytes 524320 | tf_op jit(solution)/shard_map/ppermute | solution.py:506
  111.9 1.8 shard_map.96
  119.7 2.1 %collective-permute-start.19 = (bf16[512,128]{1,0:T(8,128)(2,1)S(1)}, bf16[512,128]{1,0:T(8,128)(2,1)S(1)}, u32[]{:S(2)}, u32[]{:S(2)}) collective-permute-start(bf16[512,128]{1,0:T(8,128)(2,1)S(1)} %get-tuple-element.66), channel_id=1, source_target_pairs={{0,16},{8,24},{16,0},{24,8},{1,17},{9,25},{17,1},{25,9},{2,18},{10... | collective-permute-start | bytes 393224 | tf_op jit(solution)/shard_map/ppermute | solution.py:506
  124.9 1.9 collective-permute-start.21
  130.5 2.0 %shard_map.98 = (bf16[4,512,256]{2,1,0:T(8,128)(2,1)}, bf16[8,256,128]{2,1,0:T(8,128)(2,1)}) custom-call(s32[1]{0:T(128)} %bitcast.idx, bf16[512,256]{1,0:T(8,128)(2,1)S(1)} %get-tuple-element.65.own, bf16[512,128]{1,0:T(8,128)(2,1)S(1)} %collective-permute-done.18.r1, bf16[512,128]{1,0:T(8,128)(2,1)S(1)} %collective-permute-done.19.r2, ...), custom_call_target="tpu_custom_call" | custom-call | tf_op jit(solution)/shard_map/pallas_call | solution.py:71
  132.5 6.6 %all-to-all-start = ((bf16[8,256,128]{2,1,0:T(8,128)(2,1)}), bf16[8,256,128]{2,1,0:T(8,128)(2,1)S(1)}, u32[]{:S(2)}, u32[]{:S(2)}) async-start(bf16[8,256,128]{2,1,0:T(8,128)(2,1)} %get-tuple-element.67), calls=%async_computation | async-start | bytes 1048576 | tf_op jit(solution)/shard_map/all_to_all | solution.py:510
  144.4 6.4 %shard_map.100 = (f32[16,32,256]{2,1,0:T(8,128)}, f32[4,32,256]{2,1,0:T(8,128)}, bf16[64,256]{1,0:T(8,128)(2,1)S(1)}) custom-call(s32[1]{0:T(128)} %bitcast.idx, bf16[8,320,128]{2,1,0:T(8,128)(2,1)S(1)} %all-to-all-done.1.mine, bf16[8,320,128]{2,1,0:T(8,128)(2,1)S(1)} %collective-permute-done.25.swapped, bf16[64,256]{1,0:T(8,128)(2,1)S(1)} %get-tuple-element.71.b_other, ...), custom_call_target="tpu_custom_call" | custom-call | tf_op jit(solution)/shard_map/pallas_call | solution.py:71
  150.9 6.1 %all-to-all-done.mine = bf16[8,256,128]{2,1,0:T(8,128)(2,1)S(1)} async-done(((bf16[8,256,128]{2,1,0:T(8,128)(2,1)}), bf16[8,256,128]{2,1,0:T(8,128)(2,1)S(1)}, u32[]{:S(2)}, u32[]{:S(2)}) %all-to-all-start) | async-done | bytes 524320 | tf_op jit(solution)/shard_map/all_to_all | solution.py:510
  159.3 2.2 %collective-permute-start.28 = (f32[32,256]{1,0:T(8,128)S(1)}, f32[32,256]{1,0:T(8,128)S(1)}, u32[]{:S(2)}, u32[]{:S(2)}) collective-permute-start(f32[32,256]{1,0:T(8,128)S(1)} %shard_map.101.f0), channel_id=1, source_target_pairs={{0,16},{8,24},{16,0},{24,8},{1,17},{9,25},{17,1},{25,9},{2,18},{10... | collective-permute-start | bytes 98312 | tf_op jit(solution)/shard_map/ppermute | solution.py:506
  164.5 2.5 %shard_map.102 = (f32[4,32,256]{2,1,0:T(8,128)S(1)}, f32[8,32,256]{2,1,0:T(8,128)}) custom-call(s32[1]{0:T(128)} %bitcast.idx, f32[32,256]{1,0:T(8,128)S(1)} %shard_map.101.f0, f32[32,256]{1,0:T(8,128)S(1)} %collective-permute-done.27.f1, f32[32,256]{1,0:T(8,128)S(1)} %collective-permute-done.28.f2, f32[32,256]{1,0:T(8,128)S(1)} %collective-permute-done.29.f3, ...), custom_call_target="tpu_custom_call" | custom-call | tf_op jit(solution)/shard_map/pallas_call | solution.py:71
  167.0 3.4 %all-to-all-start.2 = ((f32[8,32,256]{2,1,0:T(8,128)}), f32[8,32,256]{2,1,0:T(8,128)S(1)}, u32[]{:S(2)}, u32[]{:S(2)}) async-start(f32[8,32,256]{2,1,0:T(8,128)} %get-tuple-element.83), calls=%async_computation.2 | async-start | bytes 524288 | tf_op jit(solution)/shard_map/all_to_all | solution.py:510
  170.5 10.1 %all-to-all-done.2.fz = f32[8,32,256]{2,1,0:T(8,128)S(1)} async-done(((f32[8,32,256]{2,1,0:T(8,128)}), f32[8,32,256]{2,1,0:T(8,128)S(1)}, u32[]{:S(2)}, u32[]{:S(2)}) %all-to-all-start.2) | async-done | bytes 262176 | tf_op jit(solution)/shard_map/all_to_all | solution.py:510
  180.6 4.6 %shard_map.103 = (f32[8,32,128]{2,1,0:T(8,128)S(1)}, f32[8,32,128]{2,1,0:T(8,128)S(1)}, f32[8,32,128]{2,1,0:T(8,128)S(1)}, f32[8,32,128]{2,1,0:T(8,128)S(1)}) custom-call(s32[1]{0:T(128)} %bitcast.idx, bf16[8,256,128]{2,1,0:T(8,128)(2,1)S(1)} %all-to-all-done.mine, bf16[8,256,128]{2,1,0:T(8,128)(2,1)S(1)} %collective-permute-done.24.swapped, ...), custom_call_target="tpu_custom_call" | custom-call | tf_op jit(solution)/shard_map/pallas_call | solution.py:71
  185.9 2.7 %collective-permute-start.31 = (f32[8,32,128]{2,1,0:T(8,128)S(1)}, f32[8,32,128]{2,1,0:T(8,128)S(1)}, u32[]{:S(2)}, u32[]{:S(2)}) collective-permute-start(f32[8,32,128]{2,1,0:T(8,128)S(1)} %get-tuple-element.89), channel_id=1, source_target_pairs={{0,2},{1,3},{2,0},{3,1},{4,6},{5,7},{6,4},{7,5},{8,10},{9,11},{10,... | collective-permute-start | bytes 393224 | tf_op jit(solution)/shard_map/ppermute | solution.py:506
  190.3 2.0 %collective-permute-done.31.p2 = f32[8,32,128]{2,1,0:T(8,128)S(1)} collective-permute-done((f32[8,32,128]{2,1,0:T(8,128)S(1)}, f32[8,32,128]{2,1,0:T(8,128)S(1)}, u32[]{:S(2)}, u32[]{:S(2)}) %collective-permute-start.31) | collective-permute-done | bytes 131104 | tf_op jit(solution)/shard_map/ppermute | solution.py:506
  (95 shorter events, 55.9 us)
Async XLA Ops:
  0.0 13.5 %collective-permute-start.3 = (bf16[16,64,256]{2,1,0:T(8,128)(2,1)}, bf16[16,64,256]{2,1,0:T(8,128)(2,1)S(1)}, u32[]{:S(2)}, u32[]{:S(2)}) collective-permute-start(bf16[16,64,256]{2,1,0:T(8,128)(2,1)} %m0.1), channel_id=1, source_target_pairs={{0,1},{1,2},{2,3},{3,0},{4,5},{5,6},{6,7},{7,4},{8,9},{9,10},{10,1... | collective-permute-start | bytes 1572872 | tf_op jit(solution)/shard_map/ppermute | solution.py:506
  2.1 25.4 %collective-permute-start.4 = (bf16[16,64,256]{2,1,0:T(8,128)(2,1)}, bf16[16,64,256]{2,1,0:T(8,128)(2,1)S(1)}, u32[]{:S(2)}, u32[]{:S(2)}) collective-permute-start(bf16[16,64,256]{2,1,0:T(8,128)(2,1)} %m0.1), channel_id=1, source_target_pairs={{0,2},{1,3},{2,0},{3,1},{4,6},{5,7},{6,4},{7,5},{8,10},{9,11},{10,... | collective-permute-start | bytes 1572872 | tf_op jit(solution)/shard_map/ppermute | solution.py:506
  4.7 23.6 %collective-permute-start.5 = (bf16[16,64,256]{2,1,0:T(8,128)(2,1)}, bf16[16,64,256]{2,1,0:T(8,128)(2,1)S(1)}, u32[]{:S(2)}, u32[]{:S(2)}) collective-permute-start(bf16[16,64,256]{2,1,0:T(8,128)(2,1)} %m0.1), channel_id=1, source_target_pairs={{0,3},{1,0},{2,1},{3,2},{4,7},{5,4},{6,5},{7,6},{8,11},{9,8},{10,9... | collective-permute-start | bytes 1572872 | tf_op jit(solution)/shard_map/ppermute | solution.py:506
  36.7 23.4 %collective-permute-start.6 = (bf16[512,256]{1,0:T(8,128)(2,1)}, bf16[512,256]{1,0:T(8,128)(2,1)}, u32[]{:S(2)}, u32[]{:S(2)}) collective-permute-start(bf16[512,256]{1,0:T(8,128)(2,1)} %get-tuple-element.53.own), channel_id=1, source_target_pairs={{0,4},{4,0},{1,5},{5,1},{2,6},{6,2},{3,7},{7,3},{8,12},{12,8},{9,1... | collective-permute-start | bytes 786440 | tf_op jit(solution)/shard_map/ppermute | solution.py:514
  45.3 6.8 %collective-permute-start.7 = (f32[8,32,128]{2,1,0:T(8,128)S(1)}, f32[8,32,128]{2,1,0:T(8,128)S(1)}, u32[]{:S(2)}, u32[]{:S(2)}) collective-permute-start(f32[8,32,128]{2,1,0:T(8,128)S(1)} %get-tuple-element.49), channel_id=1, source_target_pairs={{0,1},{1,2},{2,3},{3,0},{4,5},{5,6},{6,7},{7,4},{8,9},{9,10},{10,1... | collective-permute-start | bytes 393224 | tf_op jit(solution)/shard_map/ppermute | solution.py:506
  45.6 8.5 %collective-permute-start.8 = (f32[8,32,128]{2,1,0:T(8,128)S(1)}, f32[8,32,128]{2,1,0:T(8,128)S(1)}, u32[]{:S(2)}, u32[]{:S(2)}) collective-permute-start(f32[8,32,128]{2,1,0:T(8,128)S(1)} %get-tuple-element.50), channel_id=1, source_target_pairs={{0,2},{1,3},{2,0},{3,1},{4,6},{5,7},{6,4},{7,5},{8,10},{9,11},{10,... | collective-permute-start | bytes 393224 | tf_op jit(solution)/shard_map/ppermute | solution.py:506
  47.7 7.1 %collective-permute-start.9 = (f32[8,32,128]{2,1,0:T(8,128)S(1)}, f32[8,32,128]{2,1,0:T(8,128)S(1)}, u32[]{:S(2)}, u32[]{:S(2)}) collective-permute-start(f32[8,32,128]{2,1,0:T(8,128)S(1)} %get-tuple-element.51), channel_id=1, source_target_pairs={{0,3},{1,0},{2,1},{3,2},{4,7},{5,4},{6,5},{7,6},{8,11},{9,8},{10,9... | collective-permute-start | bytes 393224 | tf_op jit(solution)/shard_map/ppermute | solution.py:506
  61.9 6.3 %collective-permute-start.11 = (bf16[576,128]{1,0:T(8,128)(2,1)S(1)}, bf16[576,128]{1,0:T(8,128)(2,1)S(1)}, u32[]{:S(2)}, u32[]{:S(2)}) collective-permute-start(bf16[576,128]{1,0:T(8,128)(2,1)S(1)} %get-tuple-element.58), channel_id=1, source_target_pairs={{0,8},{8,16},{16,24},{24,0},{1,9},{9,17},{17,25},{25,1},{2,10},{10... | collective-permute-start | bytes 442376 | tf_op jit(solution)/shard_map/ppermute | solution.py:506
  63.1 9.2 %collective-permute-start.12 = (bf16[576,128]{1,0:T(8,128)(2,1)S(1)}, bf16[576,128]{1,0:T(8,128)(2,1)S(1)}, u32[]{:S(2)}, u32[]{:S(2)}) collective-permute-start(bf16[576,128]{1,0:T(8,128)(2,1)S(1)} %get-tuple-element.58), channel_id=1, source_target_pairs={{0,16},{8,24},{16,0},{24,8},{1,17},{9,25},{17,1},{25,9},{2,18},{10... | collective-permute-start | bytes 442376 | tf_op jit(solution)/shard_map/ppermute | solution.py:506
  65.6 8.0 %collective-permute-start.13 = (bf16[576,128]{1,0:T(8,128)(2,1)S(1)}, bf16[576,128]{1,0:T(8,128)(2,1)S(1)}, u32[]{:S(2)}, u32[]{:S(2)}) collective-permute-start(bf16[576,128]{1,0:T(8,128)(2,1)S(1)} %get-tuple-element.58), channel_id=1, source_target_pairs={{0,24},{8,0},{16,8},{24,16},{1,25},{9,1},{17,9},{25,17},{2,26},{10... | collective-permute-start | bytes 442376 | tf_op jit(solution)/shard_map/ppermute | solution.py:506
  68.2 5.4 %collective-permute-start.14 = (bf16[576,128]{1,0:T(8,128)(2,1)S(1)}, bf16[576,128]{1,0:T(8,128)(2,1)S(1)}, u32[]{:S(2)}, u32[]{:S(2)}) collective-permute-start(bf16[576,128]{1,0:T(8,128)(2,1)S(1)} %collective-permute-done.11.r1), channel_id=1, source_target_pairs={{0,4},{4,0},{1,5},{5,1},{2,6},{6,2},{3,7},{7,3},{8,12},{12,8},{9,1... | collective-permute-start | bytes 442376 | tf_op jit(solution)/shard_map/ppermute | solution.py:514
  77.3 55.3 %all-to-all-start.1 = ((bf16[8,320,128]{2,1,0:T(8,128)(2,1)}), bf16[8,320,128]{2,1,0:T(8,128)(2,1)S(1)}, u32[]{:S(2)}, u32[]{:S(2)}) async-start(bf16[8,320,128]{2,1,0:T(8,128)(2,1)} %get-tuple-element.59), calls=%async_computation.1 | async-start | bytes 1310720 | tf_op jit(solution)/shard_map/all_to_all | solution.py:510
  85.5 14.3 %collective-permute-start = (bf16[16,64,256]{2,1,0:T(8,128)(2,1)S(1)}, bf16[16,64,256]{2,1,0:T(8,128)(2,1)S(1)}, u32[]{:S(2)}, u32[]{:S(2)}) collective-permute-start(bf16[16,64,256]{2,1,0:T(8,128)(2,1)S(1)} %copy-done.8), channel_id=1, source_target_pairs={{0,1},{1,2},{2,3},{3,0},{4,5},{5,6},{6,7},{7,4},{8,9},{9,10},{10,1... | collective-permute-start | bytes 1572872 | tf_op jit(solution)/shard_map/ppermute | solution.py:506
  86.5 25.5 %collective-permute-start.1 = (bf16[16,64,256]{2,1,0:T(8,128)(2,1)S(1)}, bf16[16,64,256]{2,1,0:T(8,128)(2,1)S(1)}, u32[]{:S(2)}, u32[]{:S(2)}) collective-permute-start(bf16[16,64,256]{2,1,0:T(8,128)(2,1)S(1)} %copy-done.8), channel_id=1, source_target_pairs={{0,2},{1,3},{2,0},{3,1},{4,6},{5,7},{6,4},{7,5},{8,10},{9,11},{10,... | collective-permute-start | bytes 1572872 | tf_op jit(solution)/shard_map/ppermute | solution.py:506
  89.1 22.8 %collective-permute-start.2 = (bf16[16,64,256]{2,1,0:T(8,128)(2,1)S(1)}, bf16[16,64,256]{2,1,0:T(8,128)(2,1)S(1)}, u32[]{:S(2)}, u32[]{:S(2)}) collective-permute-start(bf16[16,64,256]{2,1,0:T(8,128)(2,1)S(1)} %copy-done.8), channel_id=1, source_target_pairs={{0,3},{1,0},{2,1},{3,2},{4,7},{5,4},{6,5},{7,6},{8,11},{9,8},{10,9... | collective-permute-start | bytes 1572872 | tf_op jit(solution)/shard_map/ppermute | solution.py:506
  116.1 2.5 %collective-permute-start.17 = (bf16[512,256]{1,0:T(8,128)(2,1)S(1)}, bf16[512,256]{1,0:T(8,128)(2,1)S(1)}, u32[]{:S(2)}, u32[]{:S(2)}) collective-permute-start(bf16[512,256]{1,0:T(8,128)(2,1)S(1)} %get-tuple-element.64.own.cown), channel_id=1, source_target_pairs={{0,4},{4,0},{1,5},{5,1},{2,6},{6,2},{3,7},{7,3},{8,12},{12,8},{9,1... | collective-permute-start | bytes 786440 | tf_op jit(solution)/shard_map/ppermute | solution.py:514
  118.9 6.0 %collective-permute-start.18 = (bf16[512,128]{1,0:T(8,128)(2,1)S(1)}, bf16[512,128]{1,0:T(8,128)(2,1)S(1)}, u32[]{:S(2)}, u32[]{:S(2)}) collective-permute-start(bf16[512,128]{1,0:T(8,128)(2,1)S(1)} %get-tuple-element.66), channel_id=1, source_target_pairs={{0,8},{8,16},{16,24},{24,0},{1,9},{9,17},{17,25},{25,1},{2,10},{10... | collective-permute-start | bytes 393224 | tf_op jit(solution)/shard_map/ppermute | solution.py:506
  119.7 8.1 %collective-permute-start.19 = (bf16[512,128]{1,0:T(8,128)(2,1)S(1)}, bf16[512,128]{1,0:T(8,128)(2,1)S(1)}, u32[]{:S(2)}, u32[]{:S(2)}) collective-permute-start(bf16[512,128]{1,0:T(8,128)(2,1)S(1)} %get-tuple-element.66), channel_id=1, source_target_pairs={{0,16},{8,24},{16,0},{24,8},{1,17},{9,25},{17,1},{25,9},{2,18},{10... | collective-permute-start | bytes 393224 | tf_op jit(solution)/shard_map/ppermute | solution.py:506
  121.8 7.3 %collective-permute-start.20 = (bf16[512,128]{1,0:T(8,128)(2,1)S(1)}, bf16[512,128]{1,0:T(8,128)(2,1)S(1)}, u32[]{:S(2)}, u32[]{:S(2)}) collective-permute-start(bf16[512,128]{1,0:T(8,128)(2,1)S(1)} %get-tuple-element.66), channel_id=1, source_target_pairs={{0,24},{8,0},{16,8},{24,16},{1,25},{9,1},{17,9},{25,17},{2,26},{10... | collective-permute-start | bytes 393224 | tf_op jit(solution)/shard_map/ppermute | solution.py:506
  124.9 4.6 %collective-permute-start.21 = (bf16[512,128]{1,0:T(8,128)(2,1)S(1)}, bf16[512,128]{1,0:T(8,128)(2,1)S(1)}, u32[]{:S(2)}, u32[]{:S(2)}) collective-permute-start(bf16[512,128]{1,0:T(8,128)(2,1)S(1)} %collective-permute-done.18.r1), channel_id=1, source_target_pairs={{0,4},{4,0},{1,5},{5,1},{2,6},{6,2},{3,7},{7,3},{8,12},{12,8},{9,1... | collective-permute-start | bytes 393224 | tf_op jit(solution)/shard_map/ppermute | solution.py:514
  127.8 2.2 %collective-permute-start.22 = (bf16[512,128]{1,0:T(8,128)(2,1)S(1)}, bf16[512,128]{1,0:T(8,128)(2,1)S(1)}, u32[]{:S(2)}, u32[]{:S(2)}) collective-permute-start(bf16[512,128]{1,0:T(8,128)(2,1)S(1)} %collective-permute-done.19.r2), channel_id=1, source_target_pairs={{0,4},{4,0},{1,5},{5,1},{2,6},{6,2},{3,7},{7,3},{8,12},{12,8},{9,1... | collective-permute-start | bytes 393224 | tf_op jit(solution)/shard_map/ppermute | solution.py:514
  132.5 24.5 %all-to-all-start = ((bf16[8,256,128]{2,1,0:T(8,128)(2,1)}), bf16[8,256,128]{2,1,0:T(8,128)(2,1)S(1)}, u32[]{:S(2)}, u32[]{:S(2)}) async-start(bf16[8,256,128]{2,1,0:T(8,128)(2,1)} %get-tuple-element.67), calls=%async_computation | async-start | bytes 1048576 | tf_op jit(solution)/shard_map/all_to_all | solution.py:510
  139.1 5.3 %collective-permute-start.25 = (bf16[8,320,128]{2,1,0:T(8,128)(2,1)S(1)}, bf16[8,320,128]{2,1,0:T(8,128)(2,1)S(1)}, u32[]{:S(2)}, u32[]{:S(2)}) collective-permute-start(bf16[8,320,128]{2,1,0:T(8,128)(2,1)S(1)} %all-to-all-done.1.mine), channel_id=1, source_target_pairs={{0,4},{4,0},{1,5},{5,1},{2,6},{6,2},{3,7},{7,3},{8,12},{12,8},{9,1... | collective-permute-start | bytes 1966088 | tf_op jit(solution)/shard_map/ppermute | solution.py:514
  150.8 6.7 %collective-permute-start.26 = (bf16[64,256]{1,0:T(8,128)(2,1)S(1)}, bf16[64,256]{1,0:T(8,128)(2,1)S(1)}, u32[]{:S(2)}, u32[]{:S(2)}) collective-permute-start(bf16[64,256]{1,0:T(8,128)(2,1)S(1)} %get-tuple-element.81.own), channel_id=1, source_target_pairs={{0,4},{4,0},{1,5},{5,1},{2,6},{6,2},{3,7},{7,3},{8,12},{12,8},{9,1... | collective-permute-start | bytes 98312 | tf_op jit(solution)/shard_map/ppermute | solution.py:514
  157.1 13.4 %collective-permute-start.24 = (bf16[8,256,128]{2,1,0:T(8,128)(2,1)S(1)}, bf16[8,256,128]{2,1,0:T(8,128)(2,1)S(1)}, u32[]{:S(2)}, u32[]{:S(2)}) collective-permute-start(bf16[8,256,128]{2,1,0:T(8,128)(2,1)S(1)} %all-to-all-done.mine), channel_id=1, source_target_pairs={{0,4},{4,0},{1,5},{5,1},{2,6},{6,2},{3,7},{7,3},{8,12},{12,8},{9,1... | collective-permute-start | bytes 1572872 | tf_op jit(solution)/shard_map/ppermute | solution.py:514
  157.8 4.2 %collective-permute-start.27 = (f32[32,256]{1,0:T(8,128)S(1)}, f32[32,256]{1,0:T(8,128)S(1)}, u32[]{:S(2)}, u32[]{:S(2)}) collective-permute-start(f32[32,256]{1,0:T(8,128)S(1)} %shard_map.101.f0), channel_id=1, source_target_pairs={{0,8},{8,16},{16,24},{24,0},{1,9},{9,17},{17,25},{25,1},{2,10},{10... | collective-permute-start | bytes 98312 | tf_op jit(solution)/shard_map/ppermute | solution.py:506
  159.3 4.3 %collective-permute-start.28 = (f32[32,256]{1,0:T(8,128)S(1)}, f32[32,256]{1,0:T(8,128)S(1)}, u32[]{:S(2)}, u32[]{:S(2)}) collective-permute-start(f32[32,256]{1,0:T(8,128)S(1)} %shard_map.101.f0), channel_id=1, source_target_pairs={{0,16},{8,24},{16,0},{24,8},{1,17},{9,25},{17,1},{25,9},{2,18},{10... | collective-permute-start | bytes 98312 | tf_op jit(solution)/shard_map/ppermute | solution.py:506
  161.4 3.1 %collective-permute-start.29 = (f32[32,256]{1,0:T(8,128)S(1)}, f32[32,256]{1,0:T(8,128)S(1)}, u32[]{:S(2)}, u32[]{:S(2)}) collective-permute-start(f32[32,256]{1,0:T(8,128)S(1)} %shard_map.101.f0), channel_id=1, source_target_pairs={{0,24},{8,0},{16,8},{24,16},{1,25},{9,1},{17,9},{25,17},{2,26},{10... | collective-permute-start | bytes 98312 | tf_op jit(solution)/shard_map/ppermute | solution.py:506
  167.0 13.6 %all-to-all-start.2 = ((f32[8,32,256]{2,1,0:T(8,128)}), f32[8,32,256]{2,1,0:T(8,128)S(1)}, u32[]{:S(2)}, u32[]{:S(2)}) async-start(f32[8,32,256]{2,1,0:T(8,128)} %get-tuple-element.83), calls=%async_computation.2 | async-start | bytes 524288 | tf_op jit(solution)/shard_map/all_to_all | solution.py:510
  185.2 5.1 %collective-permute-start.30 = (f32[8,32,128]{2,1,0:T(8,128)S(1)}, f32[8,32,128]{2,1,0:T(8,128)S(1)}, u32[]{:S(2)}, u32[]{:S(2)}) collective-permute-start(f32[8,32,128]{2,1,0:T(8,128)S(1)} %get-tuple-element.88), channel_id=1, source_target_pairs={{0,1},{1,2},{2,3},{3,0},{4,5},{5,6},{6,7},{7,4},{8,9},{9,10},{10,1... | collective-permute-start | bytes 393224 | tf_op jit(solution)/shard_map/ppermute | solution.py:506
  185.9 6.5 %collective-permute-start.31 = (f32[8,32,128]{2,1,0:T(8,128)S(1)}, f32[8,32,128]{2,1,0:T(8,128)S(1)}, u32[]{:S(2)}, u32[]{:S(2)}) collective-permute-start(f32[8,32,128]{2,1,0:T(8,128)S(1)} %get-tuple-element.89), channel_id=1, source_target_pairs={{0,2},{1,3},{2,0},{3,1},{4,6},{5,7},{6,4},{7,5},{8,10},{9,11},{10,... | collective-permute-start | bytes 393224 | tf_op jit(solution)/shard_map/ppermute | solution.py:506
  188.6 4.1 %collective-permute-start.32 = (f32[8,32,128]{2,1,0:T(8,128)S(1)}, f32[8,32,128]{2,1,0:T(8,128)S(1)}, u32[]{:S(2)}, u32[]{:S(2)}) collective-permute-start(f32[8,32,128]{2,1,0:T(8,128)S(1)} %get-tuple-element.90), channel_id=1, source_target_pairs={{0,3},{1,0},{2,1},{3,2},{4,7},{5,4},{6,5},{7,6},{8,11},{9,8},{10,9... | collective-permute-start | bytes 393224 | tf_op jit(solution)/shard_map/ppermute | solution.py:506
  (23 other events, 102.6 us)
